TPU v7x, 32 devices: a whole 2x2x4 slice. The times are simulated.
32 devices in a mesh: tower: 4 (over y, x), member: 8 (over z, core).
Axes of the slice: x: 2, y: 2, z: 4, core: 2. Of those that a mesh axis runs over, the one named last changes fastest.
Arguments:
- bag_ids: int32 [8, 8, 4, 512], P('tower', 'member'), may hold values from 0 to 511
- touch_ids: int32 [8, 8, 128], P('tower', 'member'), may hold values from 0 to 511, as said below
- elapsed: int32 [8, 8, 128], P('tower', 'member'), may hold values from 0 to 39
- tables: float32 [8, 8, 512, 64], P('tower', 'member'), may hold values from -3 to 3
- accumulator: float32 [8, 8, 512], P('tower', 'member'), may hold values from 0.001 to 0.1
- first_weight: float32 [512, 8, 1024], P(None, 'tower'), may hold values from -0.25 to 0.25
- second_weight: float32 [1024, 8, 256], P(None, 'tower'), may hold values from -0.1875 to 0.1875
- lift_weight: float32 [2048, 128], replicated, may hold values from -0.5 to 0.5
- press_weight: float32 [2048, 128], replicated, may hold values from -0.125 to 0.125
- head_weight: float32 [2048], replicated, may hold values from -0.125 to 0.125
- labels: int32 [8, 64], P('member'), may hold values 0 or 1
Outputs:
- new_tables: float32 [8, 8, 512, 64], P('tower', 'member')
- new_accumulator: float32 [8, 8, 512], P('tower', 'member')
- grad_first: float32 [512, 8, 1024], P('member', 'tower')
- grad_second: float32 [1024, 8, 256], P('member', 'tower')
- grad_lift: float32 [2048, 128], P(('tower', 'member'))
- grad_press: float32 [2048, 128], P(('tower', 'member'))
- logits: float32 [8, 64], P('member', 'tower')
Inputs may be any that keep to these rules, and one draw needn't show every extreme that they name: `touch_ids`: distinct within each table.
All inputs are finite; a program needn't handle non-finite values. No bound on the sum of `labels` on one device may be relied on, other than what follows from the above.
Results may differ from a plain program's by a relative error of at most 0.0003.
Values sent between devices are 32-bit elements; how exact they have to be, the bound alone decides.
A program may use at most 128 MiB of HBM per device.

v0:
```python
import functools
import math

import jax
import jax.numpy as jnp
from jax import lax
from jax.experimental import pallas as pl
from jax.experimental.pallas import tpu as pltpu
from jax.sharding import PartitionSpec as P

MESH = pl.DeviceIdType.MESH
DECAY_RATE = 0.98
LEARN_RATE = 1.0
EPSILON = 1e-08
F32 = jnp.float32
BF16 = jnp.bfloat16
NN = (((1,), (0,)), ((), ()))
NT = (((1,), (1,)), ((), ()))


def split(x):
    hi = x.astype(BF16)
    return hi, (x - hi.astype(F32)).astype(BF16)


def dot1(a, b, dims=NN):
    return lax.dot_general(a, b, dims, preferred_element_type=F32)


def dot3(a, b, dims=NN):
    (ah, al), (bh, bl) = a, b
    return dot1(ah, bh, dims) + (dot1(ah, bl, dims) + dot1(al, bh, dims))


def deep3(a, b):
    (ah, al), (bh, bl) = a, b
    return dot1(jnp.concatenate([ah, al, ah], axis=1), jnp.concatenate([bh, bh, bl], axis=0))


def sigmoid(x):
    return 1.0 / (1.0 + jnp.exp(-x))


def gather_kernel(
    dims,
    bag_ref,
    touch_ref,
    elapsed_ref,
    tables_ref,
    first_hbm,
    second_hbm,
    lift_hbm,
    press_hbm,
    head_ref,
    label_ref,
    logits_ref,
    decayed_ref,
    pooled_out,
    hidden_out,
    gath_out,
    counts_out,
    w2h_out,
    w2l_out,
    tower_out_hbm,
    w1h,
    w1l,
    w2f,
    w2h,
    w2l,
    lift,
    press,
    cols,
    counts_ref,
    feats,
    hidden,
    tower_out,
    own_feats,
    oa_send,
    oa_recv,
    stats,
    rs_buf,
    gath,
    load_sem,
    store_sem,
    hidden_sem,
    ag_send,
    ag_recv,
    rs_send,
    rs_recv,
    gm_send,
    gm_recv,
    gt_send,
    gt_recv,
):
    n, nt = dims
    me = lax.axis_index("member")
    tpos = lax.axis_index("tower")
    towers, bags, total = bag_ref.shape
    width, rows = tables_ref.shape[1:]
    touches = touch_ref.shape[2]
    hid, outs = w2h.shape[1:]
    fin = w1h.shape[1]
    rank = lift.shape[1]
    flat = towers * outs
    own = total // n
    piece = own // nt
    chunk = min(256, total)
    chips = n // 2
    chip, core = me // 2, lax.rem(me, 2)

    loads = []

    def load(source, target):
        loads.append(pltpu.make_async_copy(source, target, load_sem.at[len(loads)]))
        loads[-1].start()

    for t in range(towers):
        load(first_hbm.at[:, t, :], hidden.at[t, :fin])
        load(second_hbm.at[:, t, :], w2f.at[t])
    load(lift_hbm.at[pl.ds(tpos * flat, flat)], lift)
    load(press_hbm.at[pl.ds(tpos * flat, flat)], press)

    barrier = pltpu.get_barrier_semaphore()
    for d in range(1, n):
        pl.semaphore_signal(
            barrier, inc=1, device_id={"member": lax.rem(me + d, n)}, device_id_type=MESH
        )
    for d in range(1, nt):
        pl.semaphore_signal(
            barrier, inc=1, device_id={"tower": lax.rem(tpos + d, nt)}, device_id_type=MESH
        )

    stack = [bag_ref[t].astype(F32) for t in range(towers)]
    stack.append(jnp.zeros((128 - towers * bags, total), F32))
    cols[...] = jnp.concatenate(stack, axis=0).T
    stack = []
    for t in range(towers):
        stack.append(touch_ref[t].astype(F32))
        stack.append(jnp.exp(elapsed_ref[t].astype(F32) * math.log(DECAY_RATE)))
    stack.append(jnp.zeros((128 - 2 * towers, touches), F32))
    owed = jnp.concatenate(stack, axis=0).T
    pairs = []
    place = lax.broadcasted_iota(jnp.int32, (touches, rows), 1).astype(F32)
    for t in range(towers):
        ids, rates = owed[:, 2 * t : 2 * t + 1], owed[:, 2 * t + 1 : 2 * t + 2]
        chosen = jnp.sum(jnp.where(place == ids, rates, 0.0), axis=0, keepdims=True)
        decayed = tables_ref[t] * jnp.where(chosen > 0.0, chosen, 1.0)
        decayed_ref[t] = decayed
        pairs.append(jnp.concatenate(split(decayed), axis=0))
    for c in range(total // chunk):
        span = pl.ds(c * chunk, chunk)
        place = lax.broadcasted_iota(jnp.int32, (chunk, rows), 1).astype(F32)
        pooled = []
        for t in range(towers):
            counts = jnp.zeros((chunk, rows), F32)
            for b in range(bags):
                k = t * bags + b
                counts = counts + jnp.where(place == cols[span, k : k + 1], 1.0, 0.0)
            counts = counts.astype(BF16)
            counts_ref[t, span, :] = counts
            both = dot1(counts, pairs[t], NT)
            pooled.append(both[:, :width] + both[:, width:])
        feats[me, span, :] = jnp.concatenate(pooled, axis=1)

    pl.semaphore_wait(barrier, n - 1 + nt - 1)

    def block_copy(block, lane, target):
        return pltpu.make_async_remote_copy(
            src_ref=feats.at[block],
            dst_ref=feats.at[block],
            send_sem=ag_send.at[lane, block],
            recv_sem=ag_recv.at[block],
            device_id={"member": target},
            device_id_type=MESH,
        )

    def pass_on(block, right, left):
        if right:

            @pl.when(chip + 1 < chips)
            def _():
                block_copy(block, 0, me + 2).start()

        if left:

            @pl.when(chip > 0)
            def _():
                block_copy(block, 1, me - 2).start()

        block_copy(block, 2, me + 1 - 2 * core).start()

    def sent(block, right, left):
        if right:

            @pl.when(chip + 1 < chips)
            def _():
                block_copy(block, 0, me + 2).wait_send()

        if left:

            @pl.when(chip > 0)
            def _():
                block_copy(block, 1, me - 2).wait_send()

        block_copy(block, 2, me + 1 - 2 * core).wait_send()

    def own_copy(d):
        other = lax.rem(me + d, n)
        return pltpu.make_async_remote_copy(
            src_ref=feats.at[me, pl.ds(pl.multiple_of(other * own, own), own)],
            dst_ref=own_feats.at[me],
            send_sem=oa_send.at[d],
            recv_sem=oa_recv.at[d],
            device_id={"member": other},
            device_id_type=MESH,
        )

    for d in range(1, n):
        own_copy(d).start()
    own_feats[me] = feats[me, pl.ds(pl.multiple_of(me * own, own), own), :]
    pass_on(me, True, True)

    stores = []

    def store(source, target):
        stores.append(pltpu.make_async_copy(source, target, store_sem.at[len(stores)]))
        stores[-1].start()

    store(counts_ref, counts_out)

    for copy in loads:
        copy.wait()
    for t in range(towers):

        @pl.loop(0, fin // 64)
        def _(i):
            span = pl.ds(pl.multiple_of(i * 64, 64), 64)
            w1h[t, span, :], w1l[t, span, :] = split(hidden[t, span, :])

        @pl.loop(0, hid // 128)
        def _(i):
            span = pl.ds(pl.multiple_of(i * 128, 128), 128)
            w2h[t, span, :], w2l[t, span, :] = split(w2f[t, span, :])

    store(w2h, w2h_out)
    store(w2l, w2l_out)
    store(feats.at[me], pooled_out)

    head = head_ref[:, pl.ds(pl.multiple_of(tpos * flat, flat), flat)]

    for d in range(1, n):
        own_copy(d).wait_recv()
    flat_out = []
    for t in range(towers):
        part = slice(t * width, (t + 1) * width)
        x = jnp.concatenate([own_feats[j, :, part] for j in range(n)], axis=1)
        h = deep3(split(x), (w1h[t], w1l[t]))
        flat_out.append(deep3(split(h * sigmoid(h)), (w2h[t], w2l[t])))
    flat_out = jnp.concatenate(flat_out, axis=1)
    weighted = flat_out * head
    stats[:, :rank] = deep3(split(flat_out), split(press[...]))
    stats[:, rank : 2 * rank] = deep3(split(weighted), split(lift[...]))
    stats[:, 2 * rank :] = jnp.broadcast_to(
        jnp.sum(weighted, axis=1, keepdims=True), (own, rank)
    )

    def tower_copy(d):
        other = lax.rem(tpos + d, nt)
        return pltpu.make_async_remote_copy(
            src_ref=stats.at[pl.ds(pl.multiple_of(other * piece, piece), piece)],
            dst_ref=rs_buf.at[tpos],
            send_sem=rs_send.at[d],
            recv_sem=rs_recv.at[d],
            device_id={"tower": other},
            device_id_type=MESH,
        )

    for d in range(1, nt):
        tower_copy(d).start()

    def member_copy(d):
        return pltpu.make_async_remote_copy(
            src_ref=gath.at[me, tpos],
            dst_ref=gath.at[me, tpos],
            send_sem=gm_send.at[d],
            recv_sem=gm_recv.at[d],
            device_id={"member": lax.rem(me + d, n)},
            device_id_type=MESH,
        )

    def settle():
        for d in range(1, nt):
            tower_copy(d).wait_recv()
        summed = stats[pl.ds(pl.multiple_of(tpos * piece, piece), piece), :]
        for d in range(1, nt):
            summed = summed + rs_buf[lax.rem(tpos + d, nt)]
        logit = (
            jnp.sum(summed[:, :rank] * summed[:, rank : 2 * rank], axis=1, keepdims=True)
            + summed[:, 2 * rank :]
        )
        logits_ref[...] = logit
        place = lax.broadcasted_iota(jnp.int32, (piece, own), 1)
        wanted = lax.broadcasted_iota(jnp.int32, (piece, own), 0) + tpos * piece
        clicks = jnp.where(place == wanted, label_ref[...].astype(F32), 0.0)
        error = sigmoid(logit) - jnp.sum(clicks, axis=1, keepdims=True)
        gath[me, tpos, :, :rank] = error * summed[:, :rank]
        gath[me, tpos, :, rank : 2 * rank] = error * summed[:, rank : 2 * rank]
        gath[me, tpos, :, 2 * rank :] = error

        for d in range(1, n):
            member_copy(d).start()

    def accumulate(source, fresh):
        block_copy(2 * source + 1 - core, 0, me).wait_recv()
        ins = pl.ds(pl.multiple_of(source * 2 * width, 2 * width), 2 * width)

        @pl.loop(0, total // chunk)
        def _(c):
            span = pl.ds(pl.multiple_of(c * chunk, chunk), chunk)
            even, odd = feats[2 * source, span, :], feats[2 * source + 1, span, :]
            for t in range(towers):
                part = slice(t * width, (t + 1) * width)
                x = jnp.concatenate([even[:, part], odd[:, part]], axis=1)
                h = deep3(split(x), (w1h[t, ins, :], w1l[t, ins, :]))
                if fresh:
                    hidden[t, span, :] = h
                else:
                    hidden[t, span, :] += h

    accumulate(chip, True)
    for d in range(1, chips):

        @pl.when(chip >= d)
        def _():
            block = me - 2 * d
            block_copy(block, 0, me).wait_recv()
            pass_on(block, True, False)

        @pl.when(chip + d < chips)
        def _():
            block = me + 2 * d
            block_copy(block, 0, me).wait_recv()
            pass_on(block, False, True)

        @pl.when(chip >= d)
        def _():
            accumulate(chip - d, False)

        @pl.when(chip + d < chips)
        def _():
            accumulate(chip + d, False)

        if d == 1:
            settle()

    def hidden_copy(t):
        return pltpu.make_async_copy(hidden.at[t, :total], hidden_out.at[t], hidden_sem.at[t])

    for t in range(towers):
        hidden_copy(t).start()

    def tower_chunks(t):
        @pl.loop(0, total // chunk)
        def _(c):
            span = pl.ds(pl.multiple_of(c * chunk, chunk), chunk)
            h = hidden[t, span, :]
            tower_out[t, span, :] = deep3(split(h * sigmoid(h)), (w2h[t], w2l[t]))

        store(tower_out.at[t], tower_out_hbm.at[t])

    for d in range(1, n):
        member_copy(d).wait_recv()

    def column_copy(d):
        return pltpu.make_async_remote_copy(
            src_ref=gath.at[:, tpos],
            dst_ref=gath.at[:, tpos],
            send_sem=gt_send.at[d],
            recv_sem=gt_recv.at[d],
            device_id={"tower": lax.rem(tpos + d, nt)},
            device_id_type=MESH,
        )

    for d in range(1, nt):
        column_copy(d).start()
    for t in range(towers):
        tower_chunks(t)
    for d in range(1, nt):
        column_copy(d).wait_recv()
    store(gath, gath_out)
    for d in range(1, n):
        own_copy(d).wait_send()
    for d in range(1, nt):
        tower_copy(d).wait_send()
    sent(me, True, True)
    for d in range(1, chips):

        @pl.when(chip >= d)
        def _():
            sent(me - 2 * d, True, False)

        @pl.when(chip + d < chips)
        def _():
            sent(me + 2 * d, False, True)
    for d in range(1, n):
        member_copy(d).wait_send()
    for d in range(1, nt):
        column_copy(d).wait_send()

    for t in range(towers):
        hidden_copy(t).wait()
    for copy in stores:
        copy.wait()


def update_kernel(
    dims,
    logits_ref,
    tower_out_ref,
    acc_ref,
    decayed_ref,
    first_ref,
    pooled_ref,
    gath_ref,
    w2h_ref,
    w2l_ref,
    lift_hbm,
    press_hbm,
    head_ref,
    hidden_hbm,
    counts_hbm,
    new_tables_ref,
    new_acc_ref,
    grad_first_ref,
    grad_second_ref,
    grad_lift_ref,
    grad_press_ref,
    logits_out_ref,
    lift,
    press,
    hidden,
    counts,
    act,
    gl,
    gp,
    gf,
    gsec,
    gt,
    load_sem,
    hidden_sem,
    counts_sem,
):
    n, nt = dims
    me = lax.axis_index("member")
    tpos = lax.axis_index("tower")
    towers, total, hid = hidden.shape
    width, rows = decayed_ref.shape[1:]
    outs = w2h_ref.shape[2]
    rank = lift.shape[1]
    flat = towers * outs
    own = total // n
    chunk = min(256, total)

    loads = []

    def load(source, target):
        loads.append(pltpu.make_async_copy(source, target, load_sem.at[len(loads)]))
        loads[-1].start()

    load(lift_hbm.at[pl.ds(tpos * flat, flat)], lift)
    load(press_hbm.at[pl.ds(tpos * flat, flat)], press)

    def hidden_copy(t, c):
        span = pl.ds(pl.multiple_of(c * chunk, chunk), chunk)
        return pltpu.make_async_copy(
            hidden_hbm.at[t, span], hidden.at[t, span], hidden_sem.at[t, c]
        )

    def counts_copy(t):
        return pltpu.make_async_copy(counts_hbm.at[t], counts.at[t], counts_sem.at[t])

    for t in range(towers):
        for c in range(total // chunk):
            hidden_copy(t, c).start()
        counts_copy(t).start()

    block_hid = hid // n
    window = max(block_hid, 128)
    start = pl.multiple_of((me * block_hid) // 128 * 128, 128)
    gf[...] = jnp.zeros_like(gf)
    gsec[...] = jnp.zeros_like(gsec)
    gl[...] = jnp.zeros_like(gl)
    gp[...] = jnp.zeros_like(gp)
    gt[...] = jnp.zeros_like(gt)
    members_here = chunk // own
    head = head_ref[:, pl.ds(pl.multiple_of(tpos * flat, flat), flat)]
    for copy in loads:
        copy.wait()
    lift_pair = split(lift[...])
    press_pair = split(press[...])

    for t in range(towers):
        counts_copy(t).wait()
        first = split(first_ref[:, t, :])

        @pl.loop(0, total // chunk)
        def _(c):
            hidden_copy(t, c).wait()
            span = pl.ds(pl.multiple_of(c * chunk, chunk), chunk)
            block = gath_ref[pl.ds(c * members_here, members_here)].reshape(chunk, 3 * rank)
            ep = split(block[:, :rank])
            eg = split(block[:, rank : 2 * rank])
            part = slice(t * outs, (t + 1) * outs)
            head_t = head[:, part]
            lift_t = tuple(x[part] for x in lift_pair)
            press_t = tuple(x[part] for x in press_pair)
            w2 = (w2h_ref[t], w2l_ref[t])
            error_all = block[:, 2 * rank : 2 * rank + 1]
            grad_out = head_t * (error_all + dot3(ep, lift_t, NT)) + dot3(eg, press_t, NT)
            h = hidden[t, span, :]
            sig = sigmoid(h)
            a = h * sig
            act[...] = a
            tower_out = tower_out_ref[t, span, :]
            gl[part] += dot3(split((tower_out * head_t).T), ep)
            gp[part] += dot3(split(tower_out.T), eg)
            go = split(grad_out)
            gsec[t] += dot3(split(act[:, pl.ds(start, window)].T), go)
            grad_hidden = split(dot3(go, w2, NT) * (sig * (1.0 + h * (1.0 - sig))))
            pooled = pooled_ref[span, :].T[t * width : (t + 1) * width]
            gf[t] += dot3(split(pooled), grad_hidden)
            grad_pooled = dot3(first, grad_hidden, NT)
            both = dot1(jnp.concatenate(split(grad_pooled), axis=0), counts[t, span, :])
            gt[t] += both[:width] + both[width:]

        shift = pl.multiple_of(me * block_hid - start, min(block_hid, 128))
        grad_second_ref[:, t, :] = gsec[t, pl.ds(shift, block_hid), :]
        grad_first_ref[:, t, :] = gf[t]
        g = gt[t]
        value = acc_ref[t] + jnp.mean(g * g, axis=0, keepdims=True)
        new_acc_ref[t] = value
        new_tables_ref[t] = decayed_ref[t] - LEARN_RATE * g / (jnp.sqrt(value) + EPSILON)

    own_flat = pl.ds(pl.multiple_of(me * (flat // n), flat // n), flat // n)
    grad_lift_ref[...] = gl[own_flat]
    grad_press_ref[...] = gp[own_flat]
    piece = logits_ref.shape[0]
    place = lax.broadcasted_iota(jnp.int32, (piece, piece), 1)
    wanted = lax.broadcasted_iota(jnp.int32, (piece, piece), 0)
    values = jnp.where(place == wanted, logits_ref[:, :1], 0.0)
    logits_out_ref[...] = jnp.sum(values, axis=0, keepdims=True)


def per_device(n, nt, *args):
    bag_ids, touch_ids, elapsed, tables, accumulator, first, second, lift, press, head, labels = args
    towers, _, bags, total = bag_ids.shape
    rows, width = tables.shape[2:]
    fin, _, hid = first.shape
    outs = second.shape[2]
    rank = lift.shape[1]
    flat = towers * outs
    own = total // n
    piece = own // nt
    block_hid = hid // n
    window = max(block_hid, 128)
    vmem = pl.BlockSpec(memory_space=pltpu.VMEM)
    anys = pl.BlockSpec(memory_space=pl.ANY)
    chunk = min(256, total)
    sem = pltpu.SemaphoreType.DMA
    lanes = towers * width
    shape = jax.ShapeDtypeStruct
    logits, decayed, pooled, hidden, gath, counts, w2h, w2l, tower_out = pl.pallas_call(
        functools.partial(gather_kernel, (n, nt)),
        out_shape=(
            shape((piece, rank), F32),
            shape((towers, width, rows), F32),
            shape((total, lanes), F32),
            shape((towers, total, hid), F32),
            shape((n, nt, piece, 3 * rank), F32),
            shape((towers, total, rows), BF16),
            shape((towers, hid, outs), BF16),
            shape((towers, hid, outs), BF16),
            shape((towers, total, outs), F32),
        ),
        in_specs=[vmem] * 4 + [anys] * 4 + [vmem] * 2,
        out_specs=[vmem] * 2 + [anys] * 7,
        scratch_shapes=[
            pltpu.VMEM((towers, fin, hid), BF16),
            pltpu.VMEM((towers, fin, hid), BF16),
            pltpu.VMEM((towers, hid, outs), F32),
            pltpu.VMEM((towers, hid, outs), BF16),
            pltpu.VMEM((towers, hid, outs), BF16),
            pltpu.VMEM((flat, rank), F32),
            pltpu.VMEM((flat, rank), F32),
            pltpu.VMEM((total, 128), F32),
            pltpu.VMEM((towers, total, rows), BF16),
            pltpu.VMEM((n, total, lanes), F32),
            pltpu.VMEM((towers, max(total, fin), hid), F32),
            pltpu.VMEM((towers, total, outs), F32),
            pltpu.VMEM((n, own, lanes), F32),
            sem((n,)),
            sem((n,)),
            pltpu.VMEM((own, 3 * rank), F32),
            pltpu.VMEM((nt, piece, 3 * rank), F32),
            pltpu.VMEM((n, nt, piece, 3 * rank), F32),
            sem((2 * towers + 2,)),
            sem((4 + towers + 1,)),
            sem((towers,)),
            sem((3, n)),
            sem((n,)),
            sem((nt,)),
            sem((nt,)),
            sem((n,)),
            sem((n,)),
            sem((nt,)),
            sem((nt,)),
        ],
        compiler_params=pltpu.CompilerParams(
            collective_id=0, has_side_effects=True, vmem_limit_bytes=67043328
        ),
    )(
        bag_ids[:, 0],
        touch_ids,
        elapsed,
        jnp.transpose(tables[:, 0], (0, 2, 1)),
        first,
        second,
        lift,
        press,
        head[None, :],
        labels,
    )
    out = pl.pallas_call(
        functools.partial(update_kernel, (n, nt)),
        out_shape=(
            shape((towers, width, rows), F32),
            shape((towers, 1, rows), F32),
            shape((width, towers, hid), F32),
            shape((block_hid, towers, outs), F32),
            shape((flat // n, rank), F32),
            shape((flat // n, rank), F32),
            shape((1, piece), F32),
        ),
        grid=(1,),
        in_specs=[vmem] * 4
        + [pl.BlockSpec((width, towers, hid), lambda i: (lax.axis_index("member"), 0, 0))]
        + [vmem] * 4
        + [anys] * 2
        + [vmem]
        + [anys] * 2,
        out_specs=[vmem] * 7,
        scratch_shapes=[
            pltpu.VMEM((flat, rank), F32),
            pltpu.VMEM((flat, rank), F32),
            pltpu.VMEM((towers, total, hid), F32),
            pltpu.VMEM((towers, total, rows), BF16),
            pltpu.VMEM((chunk, hid), F32),
            pltpu.VMEM((flat, rank), F32),
            pltpu.VMEM((flat, rank), F32),
            pltpu.VMEM((towers, width, hid), F32),
            pltpu.VMEM((towers, window, outs), F32),
            pltpu.VMEM((towers, width, rows), F32),
            sem((2,)),
            sem((towers, total // chunk)),
            sem((towers,)),
        ],
        compiler_params=pltpu.CompilerParams(vmem_limit_bytes=67043328),
    )(
        logits,
        tower_out,
        accumulator,
        decayed,
        first,
        pooled,
        gath,
        w2h,
        w2l,
        lift,
        press,
        head[None, :],
        hidden,
        counts,
    )
    new_tables, new_acc, grad_first, grad_second, grad_lift, grad_press, logits = out
    return (
        jnp.transpose(new_tables, (0, 2, 1))[:, None],
        new_acc,
        grad_first,
        grad_second,
        grad_lift,
        grad_press,
        logits,
    )


def solution(mesh):
    placed = (
        P("tower", "member", None, None),
        P("tower", "member", None),
        P("tower", "member", None),
        P("tower", "member", None, None),
        P("tower", "member", None),
        P(None, "tower", None),
        P(None, "tower", None),
        P(),
        P(),
        P(),
        P("member", None),
    )
    return jax.shard_map(
        functools.partial(per_device, mesh.shape["member"], mesh.shape["tower"]),
        mesh=mesh,
        in_specs=placed,
        out_specs=(
            P("tower", "member", None, None),
            P("tower", "member", None),
            P("member", "tower", None),
            P("member", "tower", None),
            P(("tower", "member"), None),
            P(("tower", "member"), None),
            P("member", "tower"),
        ),
        check_vma=False,
    )
```

profile of v0, /device:TPU:1, one launch (start us, length us, event | category | flops | bytes accessed | tf_op | source)
XLA Modules:
  0.0 68.3 jit_solution(2102118203686940215)
XLA Ops:
  0.6 49.9 %shard_map.162 = (f32[16,128]{1,0:T(8,128)}, f32[2,64,512]{2,1,0:T(8,128)}, f32[512,128]{1,0:T(8,128)}, f32[2,512,1024]{2,1,0:T(8,128)}, f32[8,4,16,384]{3,2,1,0...) custom-call(s32[2,4,512]{2,1,0:T(4,128)} %bitcast.13, ...), custom_call_target="tpu_custom_call" | custom-call | tf_op jit(solution)/shard_map/pallas_call | solution.py:572
  50.6 17.6 %shard_map.163 = (f32[2,64,512]{2,1,0:T(8,128)}, f32[2,1,512]{2,1,0:T(1,128)}, f32[64,2,1024]{2,1,0:T(2,128)}, f32[128,2,256]{2,1,0:T(2,128)}, f32[64,128]{1,0:T...) custom-call(f32[16,128]{1,0:T(8,128)} %get-tuple-element.23.logits_ref, f32[2,512,256]{2,1,0:T(8,128)} %get-tuple-element.24.tower_out_ref, ...), custom_call_target="tpu_custom_call" | custom-call | tf_op jit(solution)/shard_map/pallas_call | solution.py:633
where the time goes:
time: 68.5 us; the launch traced here: 68.3 us
  Pallas kernels  67.5 us (99%)
  between operations  0.8 us (1%)
    pallas_call x1, Pallas kernels, per_device(): pl.pallas_call(functools.partial(gather_kernel, (n, nt)), out_shape=(shap...  49.9 us
    pallas_call x1, Pallas kernels, per_device(): pl.pallas_call(functools.partial(update_kernel, (n, nt)), out_shape=(shap...  17.6 us

commit v1 on v0

v1 whole, which is shorter than its diff:
```python
import functools
import math

import jax
import jax.numpy as jnp
from jax import lax
from jax.experimental import pallas as pl
from jax.experimental.pallas import tpu as pltpu
from jax.sharding import PartitionSpec as P

MESH = pl.DeviceIdType.MESH
DECAY_RATE = 0.98
LEARN_RATE = 1.0
EPSILON = 1e-08
F32 = jnp.float32
BF16 = jnp.bfloat16
NN = (((1,), (0,)), ((), ()))
NT = (((1,), (1,)), ((), ()))


def split(x):
    hi = x.astype(BF16)
    return hi, (x - hi.astype(F32)).astype(BF16)


def dot1(a, b, dims=NN):
    return lax.dot_general(a, b, dims, preferred_element_type=F32)


def few3(a, b, dims=NN):
    (ah, al), (bh, bl) = a, b
    both = dot1(jnp.concatenate([ah, al], axis=0), bh, dims)
    m = ah.shape[0]
    return both[:m] + (both[m:] + dot1(ah, bl, dims))


def deep3(a, b, dims=NN):
    (ah, al), (bh, bl) = a, b
    return dot1(
        jnp.concatenate([ah, al, ah], axis=1),
        jnp.concatenate([bh, bh, bl], axis=dims[0][1][0]),
        dims,
    )


def sigmoid(x):
    return 1.0 / (1.0 + jnp.exp(-x))


def main_kernel(
    dims,
    bag_ref,
    touch_ref,
    elapsed_ref,
    tables_ref,
    first_hbm,
    second_hbm,
    lift_hbm,
    press_hbm,
    head_ref,
    label_ref,
    logits_out,
    decayed_out,
    gt_out,
    gf_out,
    gsec_out,
    glp_out,
    stage,
    w1h,
    w1l,
    w2f,
    w2h,
    w2l,
    lift,
    press,
    mixh,
    mixl,
    cols,
    counts_ref,
    decayed,
    pool,
    feats,
    tout_send,
    tout_recv,
    stats,
    rs_buf,
    gath,
    act,
    acth,
    actl,
    pth,
    ptl,
    gf,
    gf_in,
    gsec,
    gsec_in,
    gpool,
    gpool_in,
    glp,
    glp_in,
    gt,
    logits,
    load_sem,
    store_sem,
    crit_send,
    crit_recv,
    bulk_send,
    bulk_recv,
    relay_send,
    mate_sem,
    rs_send,
    rs_recv,
    to_send,
    to_recv,
    gm_send,
    gm_recv,
    gt_send,
    gt_recv,
    back_send,
    back_recv,
):
    n, nt = dims
    me = lax.axis_index("member")
    tpos = lax.axis_index("tower")
    towers, bags, total = bag_ref.shape
    width, rows = tables_ref.shape[1:]
    touches = touch_ref.shape[2]
    hid, outs = w2h.shape[1:]
    fin = w1h.shape[1]
    rank = lift.shape[1]
    flat = towers * outs
    chips = n // 2
    own = total // n
    half = own * chips
    piece = own // nt
    chunk = min(256, half)
    tile = min(256, hid)
    pair_hid = 2 * (hid // n)
    block_hid = hid // n
    pair_flat = flat // chips
    chip, core = me // 2, lax.rem(me, 2)
    mate = me + 1 - 2 * core

    loads = []

    def load(source, target):
        loads.append(pltpu.make_async_copy(source, target, load_sem.at[len(loads)]))
        loads[-1].start()

    for t in range(towers):
        load(first_hbm.at[:, t, :], stage.at[t, :fin])
    for t in range(towers):
        load(second_hbm.at[:, t, :], w2f.at[t])
    load(lift_hbm.at[pl.ds(tpos * flat, flat)], lift)
    load(press_hbm.at[pl.ds(tpos * flat, flat)], press)

    barrier = pltpu.get_barrier_semaphore()
    for d in range(1, n):
        pl.semaphore_signal(
            barrier, inc=1, device_id={"member": lax.rem(me + d, n)}, device_id_type=MESH
        )
    for d in range(1, nt):
        pl.semaphore_signal(
            barrier, inc=1, device_id={"tower": lax.rem(tpos + d, nt)}, device_id_type=MESH
        )

    stores = []

    def store(source, target):
        stores.append(pltpu.make_async_copy(source, target, store_sem.at[len(stores)]))
        stores[-1].start()

    def slice_at(index):
        return pl.ds(pl.multiple_of(index * own, own), own)

    stack = [bag_ref[t].astype(F32) for t in range(towers)]
    stack.append(jnp.zeros((128 - towers * bags, total), F32))
    cols[...] = jnp.concatenate(stack, axis=0).T
    stack = []
    for t in range(towers):
        stack.append(touch_ref[t].astype(F32))
        stack.append(jnp.exp(elapsed_ref[t].astype(F32) * math.log(DECAY_RATE)))
    stack.append(jnp.zeros((128 - 2 * towers, touches), F32))
    owed = jnp.concatenate(stack, axis=0).T
    pairs = []
    place = lax.broadcasted_iota(jnp.int32, (touches, rows), 1).astype(F32)
    for t in range(towers):
        ids, rates = owed[:, 2 * t : 2 * t + 1], owed[:, 2 * t + 1 : 2 * t + 2]
        chosen = jnp.sum(jnp.where(place == ids, rates, 0.0), axis=0, keepdims=True)
        value = tables_ref[t] * jnp.where(chosen > 0.0, chosen, 1.0)
        decayed[t] = value
        pairs.append(jnp.concatenate(split(value), axis=0))
    place = lax.broadcasted_iota(jnp.int32, (own, rows), 1).astype(F32)
    for parity in (1 - core, core):
        pooled = []
        for t in range(towers):
            pieces = []
            for c in range(chips):
                span = slice_at(2 * c + parity)
                counts = jnp.zeros((own, rows), F32)
                for b in range(bags):
                    k = t * bags + b
                    counts = counts + jnp.where(place == cols[span, k : k + 1], 1.0, 0.0)
                pieces.append(counts.astype(BF16))
            counts = jnp.concatenate(pieces, axis=0)
            counts_ref[t, parity] = counts
            both = dot1(counts, pairs[t], NT)
            pooled.append(both[:, :width] + both[:, width:])
        pool[parity] = jnp.concatenate(pooled, axis=1)
    feats[me] = pool[core]

    pl.semaphore_wait(barrier, n - 1 + nt - 1)

    def crit_copy(i, k):
        there = lax.rem(chip + i, chips)
        return pltpu.make_async_remote_copy(
            src_ref=pool.at[k, slice_at(there)],
            dst_ref=feats.at[me, slice_at(there)],
            send_sem=crit_send.at[i, k],
            recv_sem=crit_recv.at[i, core],
            device_id={"member": 2 * there + k},
            device_id_type=MESH,
        )

    def crit_wait(i, k):
        there = lax.rem(chip + chips - i, chips)
        pltpu.make_async_remote_copy(
            src_ref=feats.at[2 * there + k, slice_at(chip)],
            dst_ref=feats.at[2 * there + k, slice_at(chip)],
            send_sem=crit_send.at[i, k],
            recv_sem=crit_recv.at[i, k],
            device_id={"member": 2 * there + k},
            device_id_type=MESH,
        ).wait_recv()

    def bulk_copy(i, k, j):
        there = lax.rem(chip + i, chips)
        at = slice_at(lax.rem(there + j, chips))
        return pltpu.make_async_remote_copy(
            src_ref=pool.at[k, at],
            dst_ref=feats.at[me, at],
            send_sem=bulk_send.at[i, k, j],
            recv_sem=bulk_recv.at[i, core, j],
            device_id={"member": 2 * there + k},
            device_id_type=MESH,
        )

    def bulk_wait(i):
        there = lax.rem(chip + chips - i, chips)
        for k in range(2):
            for j in range(1, chips):
                at = slice_at(lax.rem(chip + j, chips))
                pltpu.make_async_remote_copy(
                    src_ref=feats.at[2 * there + k, at],
                    dst_ref=feats.at[2 * there + k, at],
                    send_sem=bulk_send.at[i, k, j],
                    recv_sem=bulk_recv.at[i, k, j],
                    device_id={"member": 2 * there + k},
                    device_id_type=MESH,
                ).wait_recv()

    def mate_copy():
        return pltpu.make_async_remote_copy(
            src_ref=pool.at[1 - core],
            dst_ref=feats.at[me],
            send_sem=mate_sem.at[0],
            recv_sem=mate_sem.at[1],
            device_id={"member": mate},
            device_id_type=MESH,
        )

    order = sorted(range(1, chips), key=lambda i: -min(i, chips - i))

    def bulk_each(i, act_on):
        def both():
            for k in range(2):
                for j in range(1, chips):
                    act_on(bulk_copy(i, k, j))

        if i == 1:
            pl.when(chip != chips - 1)(both)
        elif i == chips - 1:
            pl.when(chip != 0)(both)
        else:
            both()

    def relay_each(act_on):
        def over(source, target, i):
            for k in range(2):
                for j in range(1, chips):
                    at = slice_at((target + j) % chips)
                    act_on(
                        pltpu.make_async_remote_copy(
                            src_ref=feats.at[2 * source + k, at],
                            dst_ref=feats.at[2 * source + k, at],
                            send_sem=relay_send.at[k, j],
                            recv_sem=bulk_recv.at[i, k, j],
                            device_id={"member": 2 * target + core},
                            device_id_type=MESH,
                        )
                    )

        pl.when(chip == chips - 2)(lambda: over(0, chips - 1, chips - 1))
        pl.when(chip == 1)(lambda: over(chips - 1, 0, 1))

    for i in order:
        for k in range(2):
            crit_copy(i, k).start()
    mate_copy().start()
    store(decayed, decayed_out)

    for copy in loads[:towers]:
        copy.wait()
    for t in range(towers):

        @pl.loop(0, fin // 64)
        def _(i):
            span = pl.ds(pl.multiple_of(i * 64, 64), 64)
            w1h[t, span, :], w1l[t, span, :] = split(stage[t, span, :])

    for i in order:
        bulk_each(i, lambda copy: copy.start())

    for copy in loads[towers:]:
        copy.wait()
    for t in range(towers):

        @pl.loop(0, hid // 128)
        def _(i):
            span = pl.ds(pl.multiple_of(i * 128, 128), 128)
            w2h[t, span, :], w2l[t, span, :] = split(w2f[t, span, :])

    head = head_ref[:, pl.ds(pl.multiple_of(tpos * flat, flat), flat)]
    mixh[...], mixl[...] = split(jnp.concatenate([lift[...].T * head, press[...].T], axis=0))

    mate_copy().wait_recv()
    for i in order:
        for k in range(2):
            crit_wait(i, k)
    flat_out = []
    for t in range(towers):
        part = slice(t * width, (t + 1) * width)
        x = jnp.concatenate([feats[b, slice_at(chip), part] for b in range(n)], axis=1)
        h = few3(split(x), (w1h[t], w1l[t]))
        flat_out.append(few3(split(h * sigmoid(h)), (w2h[t], w2l[t])))
    flat_out = jnp.concatenate(flat_out, axis=1)
    stats[:, : 2 * rank] = few3(split(flat_out), (mixh[...], mixl[...]), NT)
    stats[:, 2 * rank :] = jnp.broadcast_to(
        jnp.sum(flat_out * head, axis=1, keepdims=True), (own, rank)
    )

    def tower_copy(d):
        other = lax.rem(tpos + d, nt)
        return pltpu.make_async_remote_copy(
            src_ref=stats.at[pl.ds(pl.multiple_of(other * piece, piece), piece)],
            dst_ref=rs_buf.at[tpos],
            send_sem=rs_send.at[d],
            recv_sem=rs_recv.at[d],
            device_id={"tower": other},
            device_id_type=MESH,
        )

    for d in range(1, nt):
        tower_copy(d).start()

    for c in range(chips):
        tout_send[c] = flat_out[:, c * pair_flat : (c + 1) * pair_flat]
    tout_recv[chip] = tout_send[chip]

    def tout_copy(i):
        there = lax.rem(chip + i, chips)
        return pltpu.make_async_remote_copy(
            src_ref=tout_send.at[there],
            dst_ref=tout_recv.at[chip],
            send_sem=to_send.at[i],
            recv_sem=to_recv.at[i],
            device_id={"member": 2 * there + core},
            device_id_type=MESH,
        )

    def member_copy(i):
        return pltpu.make_async_remote_copy(
            src_ref=gath.at[chip, tpos],
            dst_ref=gath.at[chip, tpos],
            send_sem=gm_send.at[i],
            recv_sem=gm_recv.at[i],
            device_id={"member": 2 * lax.rem(chip + i, chips) + core},
            device_id_type=MESH,
        )

    def column_copy(d):
        return pltpu.make_async_remote_copy(
            src_ref=gath.at[:, tpos],
            dst_ref=gath.at[:, tpos],
            send_sem=gt_send.at[d],
            recv_sem=gt_recv.at[d],
            device_id={"tower": lax.rem(tpos + d, nt)},
            device_id_type=MESH,
        )

    for d in range(1, nt):
        tower_copy(d).wait_recv()
    summed = stats[pl.ds(pl.multiple_of(tpos * piece, piece), piece), :]
    for d in range(1, nt):
        summed = summed + rs_buf[lax.rem(tpos + d, nt)]
    scaled, projected = summed[:, :rank], summed[:, rank : 2 * rank]
    logit = jnp.sum(projected * scaled, axis=1, keepdims=True) + summed[:, 2 * rank :]
    logits[...] = logit
    seat = lax.broadcasted_iota(jnp.int32, (piece, own), 1)
    wanted = lax.broadcasted_iota(jnp.int32, (piece, own), 0) + tpos * piece
    clicks = jnp.where(seat == wanted, label_ref[...].astype(F32), 0.0)
    error = sigmoid(logit) - jnp.sum(clicks, axis=1, keepdims=True)
    gath[chip, tpos, :, :rank] = error * projected
    gath[chip, tpos, :, rank : 2 * rank] = error * scaled
    gath[chip, tpos, :, 2 * rank :] = error
    for i in order:
        member_copy(i).start()
    store(logits, logits_out)

    via = sorted({2, chips - 2})
    for i in via:
        bulk_wait(i)
    relay_each(lambda copy: copy.start())
    for i in order:
        tout_copy(i).start()
    for i in order:
        if i not in via:
            bulk_wait(i)

    start = pl.multiple_of(chip * pair_hid, pair_hid)

    def hidden_chunk(t, c):
        part = slice(t * width, (t + 1) * width)
        span = slice(c * chunk, (c + 1) * chunk)
        x = split(jnp.concatenate([feats[b, span, part] for b in range(n)], axis=1))
        for k in range(hid // tile):
            lanes = slice(k * tile, (k + 1) * tile)
            h = deep3(x, (w1h[t, :, lanes], w1l[t, :, lanes]))
            sig = sigmoid(h)
            a = h * sig
            act[span, lanes] = a
            stage[t, span, lanes] = sig + a * (1.0 - sig)
        both = jnp.concatenate([feats[2 * chip + k, span, part] for k in range(2)], axis=1)
        pth[t, :, span], ptl[t, :, span] = split(both.T)
        acth[t, :, span], actl[t, :, span] = split(act[span, pl.ds(start, pair_hid)].T)

    for t in range(towers):
        for c in range(half // chunk):
            hidden_chunk(t, c)
        if t == 0:
            for i in order:
                member_copy(i).wait_recv()
            for d in range(1, nt):
                column_copy(d).start()

    for i in order:
        tout_copy(i).wait_recv()
    for d in range(1, nt):
        column_copy(d).wait_recv()

    def back_copy(slot, source, target):
        return pltpu.make_async_remote_copy(
            src_ref=source,
            dst_ref=target,
            send_sem=back_send.at[slot],
            recv_sem=back_recv.at[slot],
            device_id={"member": mate},
            device_id_type=MESH,
        )

    def rows_of(which, size):
        return pl.ds(pl.multiple_of(which * size, size), size)

    def back_copies(t):
        return [
            back_copy(3 * t, gpool.at[t, rows_of(1 - core, width)], gpool_in.at[t]),
            back_copy(3 * t + 1, gf.at[t, rows_of(1 - core, width)], gf_in.at[t]),
            back_copy(3 * t + 2, gsec.at[t, rows_of(1 - core, block_hid)], gsec_in.at[t]),
        ]

    def lift_copy():
        return back_copy(3 * towers, glp.at[rows_of(1 - core, pair_flat // 2)], glp_in)

    def put(ref, index, value, fresh):
        if fresh:
            ref[index] = value
        else:
            ref[index] += value

    pair_rows = pl.ds(pl.multiple_of(chip * 2 * width, 2 * width), 2 * width)
    for t in range(towers):
        part = slice(t * outs, (t + 1) * outs)
        for c in range(half // chunk):
            span = slice(c * chunk, (c + 1) * chunk)
            here = slice(c * (chunk // own), (c + 1) * (chunk // own))
            block = gath[here].reshape(chunk, 3 * rank)
            go = split(
                block[:, 2 * rank : 2 * rank + 1] * head[:, part]
                + deep3(split(block[:, : 2 * rank]), (mixh[:, part], mixl[:, part]))
            )
            grad_pooled = jnp.zeros((2 * width, chunk), F32)
            for k in range(hid // tile):
                lanes = slice(k * tile, (k + 1) * tile)
                grad_act = deep3(go, (w2h[t, lanes, :], w2l[t, lanes, :]), NT)
                grad_hidden = split(grad_act * stage[t, span, lanes])
                value = deep3((pth[t, :, span], ptl[t, :, span]), grad_hidden)
                put(gf, (t, slice(None), lanes), value, c == 0)
                first = (w1h[t, pair_rows, lanes], w1l[t, pair_rows, lanes])
                grad_pooled = grad_pooled + deep3(first, grad_hidden, NT)
            gpool[t, :, span] = grad_pooled
            put(gsec, (t,), deep3((acth[t, :, span], actl[t, :, span]), go), c == 0)
        for copy in back_copies(t):
            copy.start()

    outputs = jnp.concatenate([tout_recv[c] for c in range(chips)], axis=0)
    block = gath[...].reshape(half, 3 * rank)
    value = deep3(split(outputs.T), split(block[:, : 2 * rank]))
    seat = lax.broadcasted_iota(jnp.int32, (pair_flat, flat), 1)
    wanted = lax.broadcasted_iota(jnp.int32, (pair_flat, flat), 0) + chip * pair_flat
    weights = jnp.sum(jnp.where(seat == wanted, head, 0.0), axis=1, keepdims=True)
    glp[:, :rank] = weights * value[:, :rank]
    glp[:, rank:] = value[:, rank:]
    lift_copy().start()

    for t in range(towers):
        from_mate = back_copies(t)
        mine = jnp.concatenate(split(gpool[t, rows_of(core, width), :]), axis=0)
        both = dot1(mine, counts_ref[t, core])
        from_mate[0].wait_recv()
        theirs = jnp.concatenate(split(gpool_in[t]), axis=0)
        both = both + dot1(theirs, counts_ref[t, 1 - core])
        gt[t] = both[:width] + both[width:]
        store(gt.at[t], gt_out.at[t])
        from_mate[1].wait_recv()
        gf_in[t] += gf[t, rows_of(core, width), :]
        store(gf_in.at[t], gf_out.at[t])
        from_mate[2].wait_recv()
        gsec_in[t] += gsec[t, rows_of(core, block_hid), :]
        store(gsec_in.at[t], gsec_out.at[t])
    lift_copy().wait_recv()
    glp_in[...] += glp[rows_of(core, pair_flat // 2), :]
    store(glp_in, glp_out)

    for i in order:
        for k in range(2):
            crit_copy(i, k).wait_send()
        bulk_each(i, lambda copy: copy.wait_send())
        tout_copy(i).wait_send()
        member_copy(i).wait_send()
    relay_each(lambda copy: copy.wait_send())
    mate_copy().wait_send()
    for d in range(1, nt):
        tower_copy(d).wait_send()
        column_copy(d).wait_send()
    for t in range(towers):
        for copy in back_copies(t):
            copy.wait_send()
    lift_copy().wait_send()
    for copy in stores:
        copy.wait()


def final_kernel(
    logits_ref,
    decayed_ref,
    gt_ref,
    gf_ref,
    gsec_ref,
    glp_ref,
    acc_ref,
    new_tables_ref,
    new_acc_ref,
    grad_first_ref,
    grad_second_ref,
    grad_lift_ref,
    grad_press_ref,
    logits_out_ref,
):
    rank = logits_ref.shape[1]
    for t in range(gt_ref.shape[0]):
        grad_second_ref[:, t, :] = gsec_ref[t]
        grad_first_ref[:, t, :] = gf_ref[t]
        g = gt_ref[t]
        value = acc_ref[t] + jnp.mean(g * g, axis=0, keepdims=True)
        new_acc_ref[t] = value
        new_tables_ref[t] = decayed_ref[t] - LEARN_RATE * g / (jnp.sqrt(value) + EPSILON)
    grad_lift_ref[...] = glp_ref[:, :rank]
    grad_press_ref[...] = glp_ref[:, rank:]
    piece = logits_ref.shape[0]
    place = lax.broadcasted_iota(jnp.int32, (piece, piece), 1)
    wanted = lax.broadcasted_iota(jnp.int32, (piece, piece), 0)
    values = jnp.where(place == wanted, logits_ref[:, :1], 0.0)
    logits_out_ref[...] = jnp.sum(values, axis=0, keepdims=True)


def per_device(n, nt, *args):
    bag_ids, touch_ids, elapsed, tables, accumulator, first, second, lift, press, head, labels = args
    towers, _, bags, total = bag_ids.shape
    rows, width = tables.shape[2:]
    fin, _, hid = first.shape
    outs = second.shape[2]
    rank = lift.shape[1]
    flat = towers * outs
    chips = n // 2
    own = total // n
    half = own * chips
    piece = own // nt
    block_hid = hid // n
    pair_flat = flat // chips
    lanes = towers * width
    vmem = pl.BlockSpec(memory_space=pltpu.VMEM)
    anys = pl.BlockSpec(memory_space=pl.ANY)
    sem = pltpu.SemaphoreType.DMA
    shape = jax.ShapeDtypeStruct
    between = pl.pallas_call(
        functools.partial(main_kernel, (n, nt)),
        out_shape=(
            shape((piece, rank), F32),
            shape((towers, width, rows), F32),
            shape((towers, width, rows), F32),
            shape((towers, width, hid), F32),
            shape((towers, block_hid, outs), F32),
            shape((pair_flat // 2, 2 * rank), F32),
        ),
        in_specs=[vmem] * 4 + [anys] * 4 + [vmem] * 2,
        out_specs=[anys] * 6,
        scratch_shapes=[
            pltpu.VMEM((towers, max(half, fin), hid), F32),
            pltpu.VMEM((towers, fin, hid), BF16),
            pltpu.VMEM((towers, fin, hid), BF16),
            pltpu.VMEM((towers, hid, outs), F32),
            pltpu.VMEM((towers, hid, outs), BF16),
            pltpu.VMEM((towers, hid, outs), BF16),
            pltpu.VMEM((flat, rank), F32),
            pltpu.VMEM((flat, rank), F32),
            pltpu.VMEM((2 * rank, flat), BF16),
            pltpu.VMEM((2 * rank, flat), BF16),
            pltpu.VMEM((total, 128), F32),
            pltpu.VMEM((towers, 2, half, rows), BF16),
            pltpu.VMEM((towers, width, rows), F32),
            pltpu.VMEM((2, half, lanes), F32),
            pltpu.VMEM((n, half, lanes), F32),
            pltpu.VMEM((chips, own, pair_flat), F32),
            pltpu.VMEM((chips, own, pair_flat), F32),
            pltpu.VMEM((own, 3 * rank), F32),
            pltpu.VMEM((nt, piece, 3 * rank), F32),
            pltpu.VMEM((chips, nt, piece, 3 * rank), F32),
            pltpu.VMEM((half, hid), F32),
            pltpu.VMEM((towers, 2 * block_hid, half), BF16),
            pltpu.VMEM((towers, 2 * block_hid, half), BF16),
            pltpu.VMEM((towers, 2 * width, half), BF16),
            pltpu.VMEM((towers, 2 * width, half), BF16),
            pltpu.VMEM((towers, 2 * width, hid), F32),
            pltpu.VMEM((towers, width, hid), F32),
            pltpu.VMEM((towers, 2 * block_hid, outs), F32),
            pltpu.VMEM((towers, block_hid, outs), F32),
            pltpu.VMEM((towers, 2 * width, half), F32),
            pltpu.VMEM((towers, width, half), F32),
            pltpu.VMEM((pair_flat, 2 * rank), F32),
            pltpu.VMEM((pair_flat // 2, 2 * rank), F32),
            pltpu.VMEM((towers, width, rows), F32),
            pltpu.VMEM((piece, rank), F32),
            sem((2 * towers + 2,)),
            sem((3 + 3 * towers,)),
            sem((chips, 2)),
            sem((chips, 2)),
            sem((chips, 2, chips)),
            sem((chips, 2, chips)),
            sem((2, chips)),
            sem((2,)),
            sem((nt,)),
            sem((nt,)),
            sem((chips,)),
            sem((chips,)),
            sem((chips,)),
            sem((chips,)),
            sem((nt,)),
            sem((nt,)),
            sem((3 * towers + 1,)),
            sem((3 * towers + 1,)),
        ],
        compiler_params=pltpu.CompilerParams(
            collective_id=0, has_side_effects=True, vmem_limit_bytes=67043328
        ),
    )(
        bag_ids[:, 0],
        touch_ids,
        elapsed,
        jnp.transpose(tables[:, 0], (0, 2, 1)),
        first,
        second,
        lift,
        press,
        head[None, :],
        labels,
    )
    out = pl.pallas_call(
        final_kernel,
        out_shape=(
            shape((towers, width, rows), F32),
            shape((towers, 1, rows), F32),
            shape((width, towers, hid), F32),
            shape((block_hid, towers, outs), F32),
            shape((flat // n, rank), F32),
            shape((flat // n, rank), F32),
            shape((1, piece), F32),
        ),
        in_specs=[vmem] * 7,
        out_specs=[vmem] * 7,
    )(*between, accumulator)
    new_tables, new_acc, grad_first, grad_second, grad_lift, grad_press, logits = out
    return (
        jnp.transpose(new_tables, (0, 2, 1))[:, None],
        new_acc,
        grad_first,
        grad_second,
        grad_lift,
        grad_press,
        logits,
    )


def solution(mesh):
    placed = (
        P("tower", "member", None, None),
        P("tower", "member", None),
        P("tower", "member", None),
        P("tower", "member", None, None),
        P("tower", "member", None),
        P(None, "tower", None),
        P(None, "tower", None),
        P(),
        P(),
        P(),
        P("member", None),
    )
    return jax.shard_map(
        functools.partial(per_device, mesh.shape["member"], mesh.shape["tower"]),
        mesh=mesh,
        in_specs=placed,
        out_specs=(
            P("tower", "member", None, None),
            P("tower", "member", None),
            P("member", "tower", None),
            P("member", "tower", None),
            P(("tower", "member"), None),
            P(("tower", "member"), None),
            P("member", "tower"),
        ),
        check_vma=False,
    )
```

time: 68.5 us -> 50.1 us (0.73)
  Pallas kernels: 67.5 us -> 49.3 us
    pallas_call x2, Pallas kernels: 67.5 us -> 49.3 us  [the longest x1 46.9 us: per_device(): pl.pallas_call(functools.partial(main_kernel, (n, nt)), out_shape=(shape(...]
where the time goes in v1:
time: 50.1 us; the launch traced here: 50 us
  Pallas kernels  49.3 us (98%)
  between operations  0.64 us (1%)
    pallas_call x1, Pallas kernels, per_device(): pl.pallas_call(functools.partial(main_kernel, (n, nt)), out_shape=(shape(...  46.9 us
    pallas_call x1, Pallas kernels, per_device(): pl.pallas_call(final_kernel, out_shape=(shape((towers, width, rows), F32)...  2.4 us

profile of v1, /device:TPU:1, one launch (start us, length us, event | category | flops | bytes accessed | tf_op | source)
XLA Modules:
  0.0 50.0 jit_solution(13056103698173597919)
XLA Ops:
  0.6 46.9 %shard_map.162 = (f32[16,128]{1,0:T(8,128)}, f32[2,64,512]{2,1,0:T(8,128)}, f32[2,64,512]{2,1,0:T(8,128)}, f32[2,64,1024]{2,1,0:T(8,128)}, f32[2,128,256]{2,1,0:T(8,128)}, /*index=5*/f32[64,256]{1,0:T(8,128)}) custom-call(s32[2,4,512]{2,1,0:T(4,128)} %bitcast.11, s32[2,1,128]{2,1,0:T(1,128)} %touch_ref.1, s32[2,1,128]{2,1,0:T(1,128)} %elapsed_ref.1, ...), custom_call_target="tpu_custom_call" | custom-call | tf_op jit(solution)/shard_map/pallas_call | solution.py:615
  47.6 2.4 %shard_map.163 = (f32[2,64,512]{2,1,0:T(8,128)}, f32[2,1,512]{2,1,0:T(1,128)}, f32[64,2,1024]{2,1,0:T(2,128)}, f32[128,2,256]{2,1,0:T(2,128)}, f32[64,128]{1,0:T...) custom-call(f32[16,128]{1,0:T(8,128)} %get-tuple-element.20.logits_ref, f32[2,64,512]{2,1,0:T(8,128)} %get-tuple-element.21.decayed_ref, ...), custom_call_target="tpu_custom_call" | custom-call | tf_op jit(solution)/shard_map/pallas_call | solution.py:697

commit v2 on v1

--- a/solution.py
+++ b/solution.py
@@ -102,12 +102,10 @@
     logits,
     load_sem,
     store_sem,
-    crit_send,
-    crit_recv,
-    bulk_send,
-    bulk_recv,
-    relay_send,
-    mate_sem,
+    own_send,
+    mate_send,
+    ag_send,
+    ag_recv,
     rs_send,
     rs_recv,
     to_send,
@@ -190,124 +188,113 @@
         value = tables_ref[t] * jnp.where(chosen > 0.0, chosen, 1.0)
         decayed[t] = value
         pairs.append(jnp.concatenate(split(value), axis=0))
-    place = lax.broadcasted_iota(jnp.int32, (own, rows), 1).astype(F32)
-    for parity in (1 - core, core):
-        pooled = []
-        for t in range(towers):
-            pieces = []
-            for c in range(chips):
-                span = slice_at(2 * c + parity)
-                counts = jnp.zeros((own, rows), F32)
-                for b in range(bags):
-                    k = t * bags + b
-                    counts = counts + jnp.where(place == cols[span, k : k + 1], 1.0, 0.0)
-                pieces.append(counts.astype(BF16))
-            counts = jnp.concatenate(pieces, axis=0)
-            counts_ref[t, parity] = counts
-            both = dot1(counts, pairs[t], NT)
-            pooled.append(both[:, :width] + both[:, width:])
-        pool[parity] = jnp.concatenate(pooled, axis=1)
-    feats[me] = pool[core]
-
-    pl.semaphore_wait(barrier, n - 1 + nt - 1)
-
-    def crit_copy(i, k):
-        there = lax.rem(chip + i, chips)
-        return pltpu.make_async_remote_copy(
-            src_ref=pool.at[k, slice_at(there)],
-            dst_ref=feats.at[me, slice_at(there)],
-            send_sem=crit_send.at[i, k],
-            recv_sem=crit_recv.at[i, core],
-            device_id={"member": 2 * there + k},
-            device_id_type=MESH,
-        )
-
-    def crit_wait(i, k):
-        there = lax.rem(chip + chips - i, chips)
-        pltpu.make_async_remote_copy(
-            src_ref=feats.at[2 * there + k, slice_at(chip)],
-            dst_ref=feats.at[2 * there + k, slice_at(chip)],
-            send_sem=crit_send.at[i, k],
-            recv_sem=crit_recv.at[i, k],
-            device_id={"member": 2 * there + k},
-            device_id_type=MESH,
-        ).wait_recv()
-
-    def bulk_copy(i, k, j):
-        there = lax.rem(chip + i, chips)
-        at = slice_at(lax.rem(there + j, chips))
+    def own_copy(sign, k, s):
+        at = slice_at(s)
         return pltpu.make_async_remote_copy(
             src_ref=pool.at[k, at],
             dst_ref=feats.at[me, at],
-            send_sem=bulk_send.at[i, k, j],
-            recv_sem=bulk_recv.at[i, core, j],
-            device_id={"member": 2 * there + k},
+            send_sem=own_send.at[(1 - sign) // 2, k, s],
+            recv_sem=ag_recv.at[me, s],
+            device_id={"member": 2 * (chip + sign) + k},
             device_id_type=MESH,
         )
 
-    def bulk_wait(i):
-        there = lax.rem(chip + chips - i, chips)
-        for k in range(2):
-            for j in range(1, chips):
-                at = slice_at(lax.rem(chip + j, chips))
-                pltpu.make_async_remote_copy(
-                    src_ref=feats.at[2 * there + k, at],
-                    dst_ref=feats.at[2 * there + k, at],
-                    send_sem=bulk_send.at[i, k, j],
-                    recv_sem=bulk_recv.at[i, k, j],
-                    device_id={"member": 2 * there + k},
-                    device_id_type=MESH,
-                ).wait_recv()
-
-    def mate_copy():
+    def mate_copy(s):
+        at = slice_at(s)
         return pltpu.make_async_remote_copy(
-            src_ref=pool.at[1 - core],
-            dst_ref=feats.at[me],
-            send_sem=mate_sem.at[0],
-            recv_sem=mate_sem.at[1],
+            src_ref=pool.at[1 - core, at],
+            dst_ref=feats.at[me, at],
+            send_sem=mate_send.at[s],
+            recv_sem=ag_recv.at[me, s],
             device_id={"member": mate},
             device_id_type=MESH,
         )
 
+    def block_copy(sign, block, s):
+        at = slice_at(s)
+        return pltpu.make_async_remote_copy(
+            src_ref=feats.at[block, at],
+            dst_ref=feats.at[block, at],
+            send_sem=ag_send.at[(1 - sign) // 2, block, s],
+            recv_sem=ag_recv.at[block, s],
+            device_id={"member": 2 * (chip + sign) + core},
+            device_id_type=MESH,
+        )
+
+    def goes_on(sign):
+        return chip < chips - 1 if sign > 0 else chip > 0
+
+    def present(sign, d):
+        return chip >= d if sign > 0 else chip + d < chips
+
+    def ahead(sign, act_on):
+        @pl.loop(0, chips - 1 - chip if sign > 0 else chip)
+        def _(i):
+            act_on(chips - 1 - i if sign > 0 else i)
+
+    def behind(sign, act_on):
+        @pl.loop(0, chip if sign > 0 else chips - 1 - chip)
+        def _(i):
+            act_on(chip - 1 - i if sign > 0 else chip + 1 + i)
+
+    def pass_on(sign, d, over):
+        def one(s):
+            for k in range(2):
+                block = 2 * (chip - sign * d) + k
+                block_copy(sign, block, s).wait_recv()
+
+                @pl.when(goes_on(sign))
+                def _():
+                    block_copy(sign, block, s).start()
+
+        @pl.when(present(sign, d))
+        def _():
+            over(one)
+
+    def own_rest(sign, over):
+        def one(s):
+            for k in range(2):
+                own_copy(sign, k, s).start()
+
+        @pl.when(goes_on(sign))
+        def _():
+            over(one)
+
     order = sorted(range(1, chips), key=lambda i: -min(i, chips - i))
-
-    def bulk_each(i, act_on):
-        def both():
+    place = lax.broadcasted_iota(jnp.int32, (2 * own, rows), 1).astype(F32)
+    for i in order + [0]:
+        there = lax.rem(chip + i, chips)
+        span = pl.ds(pl.multiple_of(there * 2 * own, 2 * own), 2 * own)
+        pooled = []
+        for t in range(towers):
+            counts = jnp.zeros((2 * own, rows), F32)
+            for b in range(bags):
+                k = t * bags + b
+                counts = counts + jnp.where(place == cols[span, k : k + 1], 1.0, 0.0)
+            counts = counts.astype(BF16)
             for k in range(2):
-                for j in range(1, chips):
-                    act_on(bulk_copy(i, k, j))
-
-        if i == 1:
-            pl.when(chip != chips - 1)(both)
-        elif i == chips - 1:
-            pl.when(chip != 0)(both)
-        else:
-            both()
-
-    def relay_each(act_on):
-        def over(source, target, i):
-            for k in range(2):
-                for j in range(1, chips):
-                    at = slice_at((target + j) % chips)
-                    act_on(
-                        pltpu.make_async_remote_copy(
-                            src_ref=feats.at[2 * source + k, at],
-                            dst_ref=feats.at[2 * source + k, at],
-                            send_sem=relay_send.at[k, j],
-                            recv_sem=bulk_recv.at[i, k, j],
-                            device_id={"member": 2 * target + core},
-                            device_id_type=MESH,
-                        )
-                    )
-
-        pl.when(chip == chips - 2)(lambda: over(0, chips - 1, chips - 1))
-        pl.when(chip == 1)(lambda: over(chips - 1, 0, 1))
-
-    for i in order:
+                counts_ref[t, k, slice_at(there), :] = counts[k * own : (k + 1) * own]
+            both = dot1(counts, pairs[t], NT)
+            pooled.append(both[:, :width] + both[:, width:])
+        pooled = jnp.concatenate(pooled, axis=1)
         for k in range(2):
-            crit_copy(i, k).start()
-    mate_copy().start()
-    store(decayed, decayed_out)
+            pool[k, slice_at(there), :] = pooled[k * own : (k + 1) * own]
+        if i == order[0]:
+            pl.semaphore_wait(barrier, n - 1 + nt - 1)
+        if i:
+
+            @pl.when(there > chip)
+            def _():
+                for k in range(2):
+                    own_copy(1, k, there).start()
+
+            @pl.when(there < chip)
+            def _():
+                for k in range(2):
+                    own_copy(-1, k, there).start()
+
+        mate_copy(there).start()
+    feats[me] = pool[core]
 
     for copy in loads[:towers]:
         copy.wait()
@@ -318,8 +305,10 @@
             span = pl.ds(pl.multiple_of(i * 64, 64), 64)
             w1h[t, span, :], w1l[t, span, :] = split(stage[t, span, :])
 
-    for i in order:
-        bulk_each(i, lambda copy: copy.start())
+    for sign in (1, -1):
+        pass_on(sign, 1, functools.partial(ahead, sign))
+    for sign in (1, -1):
+        own_rest(sign, lambda act_on: act_on(chip))
 
     for copy in loads[towers:]:
         copy.wait()
@@ -333,10 +322,20 @@
     head = head_ref[:, pl.ds(pl.multiple_of(tpos * flat, flat), flat)]
     mixh[...], mixl[...] = split(jnp.concatenate([lift[...].T * head, press[...].T], axis=0))
 
-    mate_copy().wait_recv()
-    for i in order:
-        for k in range(2):
-            crit_wait(i, k)
+    for d in range(2, chips):
+        for sign in (1, -1):
+            pass_on(sign, d, functools.partial(ahead, sign))
+    for sign in (1, -1):
+        own_rest(sign, functools.partial(behind, sign))
+    store(decayed, decayed_out)
+
+    def mate_arrives(s):
+        block_copy(1, mate, s).wait_recv()
+
+    mate_arrives(chip)
+    for d in range(1, chips):
+        for sign in (1, -1):
+            pass_on(sign, d, lambda act_on: act_on(chip))
     flat_out = []
     for t in range(towers):
         part = slice(t * width, (t + 1) * width)
@@ -397,6 +396,30 @@
             device_id={"tower": lax.rem(tpos + d, nt)},
             device_id_type=MESH,
         )
+
+    for sign in (1, -1):
+        pass_on(sign, 1, functools.partial(behind, sign))
+    for sign in (1, -1):
+        behind(sign, mate_arrives)
+    per = 4
+    together = per * width
+
+    def hidden_group(t, c, g):
+        part = slice(t * width, (t + 1) * width)
+        span = slice(c * chunk, (c + 1) * chunk)
+        x = jnp.concatenate([feats[per * g + k, span, part] for k in range(per)], axis=1)
+        x = split(x)
+        ins = pl.ds(pl.multiple_of(g * together, together), together)
+        for k in range(hid // tile):
+            lanes = slice(k * tile, (k + 1) * tile)
+            yield lanes, deep3(x, (w1h[t, ins, lanes], w1l[t, ins, lanes]))
+
+    near = chip // 2
+    for t in range(towers):
+        for c in range(half // chunk):
+            span = slice(c * chunk, (c + 1) * chunk)
+            for lanes, value in hidden_group(t, c, near):
+                stage[t, span, lanes] = value
 
     for d in range(1, nt):
         tower_copy(d).wait_recv()
@@ -417,41 +440,43 @@
         member_copy(i).start()
     store(logits, logits_out)
 
-    via = sorted({2, chips - 2})
-    for i in via:
-        bulk_wait(i)
-    relay_each(lambda copy: copy.start())
+    def far(sign, d, wanted):
+        @pl.when(wanted)
+        def _():
+            pass_on(sign, d, functools.partial(behind, sign))
+
+    for d in range(2, chips):
+        for sign in (1, -1):
+            far(sign, d, goes_on(sign))
     for i in order:
         tout_copy(i).start()
     for i in order:
-        if i not in via:
-            bulk_wait(i)
+        member_copy(i).wait_recv()
+    for d in range(1, nt):
+        column_copy(d).start()
+    for d in range(2, chips):
+        for sign in (1, -1):
+            far(sign, d, jnp.logical_not(goes_on(sign)))
 
     start = pl.multiple_of(chip * pair_hid, pair_hid)
-
-    def hidden_chunk(t, c):
+    groups = n // per
+    for t in range(towers):
         part = slice(t * width, (t + 1) * width)
-        span = slice(c * chunk, (c + 1) * chunk)
-        x = split(jnp.concatenate([feats[b, span, part] for b in range(n)], axis=1))
-        for k in range(hid // tile):
-            lanes = slice(k * tile, (k + 1) * tile)
-            h = deep3(x, (w1h[t, :, lanes], w1l[t, :, lanes]))
-            sig = sigmoid(h)
-            a = h * sig
-            act[span, lanes] = a
-            stage[t, span, lanes] = sig + a * (1.0 - sig)
-        both = jnp.concatenate([feats[2 * chip + k, span, part] for k in range(2)], axis=1)
-        pth[t, :, span], ptl[t, :, span] = split(both.T)
-        acth[t, :, span], actl[t, :, span] = split(act[span, pl.ds(start, pair_hid)].T)
-
-    for t in range(towers):
         for c in range(half // chunk):
-            hidden_chunk(t, c)
-        if t == 0:
-            for i in order:
-                member_copy(i).wait_recv()
-            for d in range(1, nt):
-                column_copy(d).start()
+            span = slice(c * chunk, (c + 1) * chunk)
+            for i in range(1, groups):
+                for lanes, value in hidden_group(t, c, lax.rem(near + i, groups)):
+                    h = stage[t, span, lanes] + value
+                    if i < groups - 1:
+                        stage[t, span, lanes] = h
+                    else:
+                        sig = sigmoid(h)
+                        a = h * sig
+                        act[span, lanes] = a
+                        stage[t, span, lanes] = sig + a * (1.0 - sig)
+            both = jnp.concatenate([feats[2 * chip + k, span, part] for k in range(2)], axis=1)
+            pth[t, :, span], ptl[t, :, span] = split(both.T)
+            acth[t, :, span], actl[t, :, span] = split(act[span, pl.ds(start, pair_hid)].T)
 
     for i in order:
         tout_copy(i).wait_recv()
@@ -541,14 +566,25 @@
     glp_in[...] += glp[rows_of(core, pair_flat // 2), :]
     store(glp_in, glp_out)
 
+    for sign in (1, -1):
+
+        @pl.when(goes_on(sign))
+        def _():
+            for s in range(chips):
+                for k in range(2):
+                    own_copy(sign, k, s).wait_send()
+                for d in range(1, chips):
+
+                    @pl.when(present(sign, d))
+                    def _():
+                        for k in range(2):
+                            block_copy(sign, 2 * (chip - sign * d) + k, s).wait_send()
+
+    for s in range(chips):
+        mate_copy(s).wait_send()
     for i in order:
-        for k in range(2):
-            crit_copy(i, k).wait_send()
-        bulk_each(i, lambda copy: copy.wait_send())
         tout_copy(i).wait_send()
         member_copy(i).wait_send()
-    relay_each(lambda copy: copy.wait_send())
-    mate_copy().wait_send()
     for d in range(1, nt):
         tower_copy(d).wait_send()
         column_copy(d).wait_send()
@@ -662,12 +698,10 @@
             pltpu.VMEM((piece, rank), F32),
             sem((2 * towers + 2,)),
             sem((3 + 3 * towers,)),
-            sem((chips, 2)),
-            sem((chips, 2)),
-            sem((chips, 2, chips)),
-            sem((chips, 2, chips)),
-            sem((2, chips)),
-            sem((2,)),
+            sem((2, 2, chips)),
+            sem((chips,)),
+            sem((2, n, chips)),
+            sem((n, chips)),
             sem((nt,)),
             sem((nt,)),
             sem((chips,)),

time: 50.1 us -> 47.8 us (0.954)
  Pallas kernels: 49.3 us -> 47 us
    pallas_call x1, Pallas kernels: 46.9 us -> 44.6 us  [per_device(): pl.pallas_call(functools.partial(main_kernel, (n, nt)), out_shape=(shape(...]
where the time goes in v2:
time: 47.8 us; the launch traced here: 47.7 us
  Pallas kernels  47 us (98%)
  between operations  0.64 us (1%)
    pallas_call x1, Pallas kernels, per_device(): pl.pallas_call(functools.partial(main_kernel, (n, nt)), out_shape=(shape(...  44.6 us
    pallas_call x1, Pallas kernels, per_device(): pl.pallas_call(final_kernel, out_shape=(shape((towers, width, rows), F32)...  2.4 us

profile of v2, /device:TPU:1, one launch (start us, length us, event | category | flops | bytes accessed | tf_op | source)
XLA Modules:
  0.0 47.7 jit_solution(13863370491498492877)
XLA Ops:
  0.6 44.6 %shard_map.162 = (f32[16,128]{1,0:T(8,128)}, f32[2,64,512]{2,1,0:T(8,128)}, f32[2,64,512]{2,1,0:T(8,128)}, f32[2,64,1024]{2,1,0:T(8,128)}, f32[2,128,256]{2,1,0:T(8,128)}, /*index=5*/f32[64,256]{1,0:T(8,128)}) custom-call(s32[2,4,512]{2,1,0:T(4,128)} %bitcast.11, s32[2,1,128]{2,1,0:T(1,128)} %touch_ref.1, s32[2,1,128]{2,1,0:T(1,128)} %elapsed_ref.1, ...), custom_call_target="tpu_custom_call" | custom-call | tf_op jit(solution)/shard_map/pallas_call | solution.py:651
  45.3 2.4 %shard_map.163 = (f32[2,64,512]{2,1,0:T(8,128)}, f32[2,1,512]{2,1,0:T(1,128)}, f32[64,2,1024]{2,1,0:T(2,128)}, f32[128,2,256]{2,1,0:T(2,128)}, f32[64,128]{1,0:T...) custom-call(f32[16,128]{1,0:T(8,128)} %get-tuple-element.20.logits_ref, f32[2,64,512]{2,1,0:T(8,128)} %get-tuple-element.21.decayed_ref, ...), custom_call_target="tpu_custom_call" | custom-call | tf_op jit(solution)/shard_map/pallas_call | solution.py:731

commit v3 on v2

--- a/solution.py
+++ b/solution.py
@@ -85,6 +85,7 @@
     stats,
     rs_buf,
     gath,
+    errs,
     act,
     acth,
     actl,
@@ -251,19 +252,25 @@
         def _():
             over(one)
 
-    def own_rest(sign, over):
+    def at_once(sign):
+        if sign > 0:
+            return jnp.logical_or(chip == 0, chip == chips - 2)
+        return jnp.logical_or(chip == chips - 1, chip == 1)
+
+    def own_rest(sign):
         def one(s):
             for k in range(2):
                 own_copy(sign, k, s).start()
 
-        @pl.when(goes_on(sign))
+        @pl.when(goes_on(sign) & jnp.logical_not(at_once(sign)))
         def _():
-            over(one)
+            one(chip)
+            behind(sign, one)
 
     order = sorted(range(1, chips), key=lambda i: -min(i, chips - i))
     place = lax.broadcasted_iota(jnp.int32, (2 * own, rows), 1).astype(F32)
-    for i in order + [0]:
-        there = lax.rem(chip + i, chips)
+    for i in range(1, chips + 1):
+        there = lax.rem(jnp.where(chip < chips // 2, chip + chips - i, chip + i), chips)
         span = pl.ds(pl.multiple_of(there * 2 * own, 2 * own), 2 * own)
         pooled = []
         for t in range(towers):
@@ -279,19 +286,18 @@
         pooled = jnp.concatenate(pooled, axis=1)
         for k in range(2):
             pool[k, slice_at(there), :] = pooled[k * own : (k + 1) * own]
-        if i == order[0]:
+        if i == 1:
             pl.semaphore_wait(barrier, n - 1 + nt - 1)
-        if i:
-
-            @pl.when(there > chip)
-            def _():
-                for k in range(2):
-                    own_copy(1, k, there).start()
-
-            @pl.when(there < chip)
-            def _():
-                for k in range(2):
-                    own_copy(-1, k, there).start()
+
+        @pl.when(jnp.logical_or(there > chip, at_once(1)) & goes_on(1))
+        def _():
+            for k in range(2):
+                own_copy(1, k, there).start()
+
+        @pl.when(jnp.logical_or(there < chip, at_once(-1)) & goes_on(-1))
+        def _():
+            for k in range(2):
+                own_copy(-1, k, there).start()
 
         mate_copy(there).start()
     feats[me] = pool[core]
@@ -308,7 +314,7 @@
     for sign in (1, -1):
         pass_on(sign, 1, functools.partial(ahead, sign))
     for sign in (1, -1):
-        own_rest(sign, lambda act_on: act_on(chip))
+        own_rest(sign)
 
     for copy in loads[towers:]:
         copy.wait()
@@ -325,8 +331,6 @@
     for d in range(2, chips):
         for sign in (1, -1):
             pass_on(sign, d, functools.partial(ahead, sign))
-    for sign in (1, -1):
-        own_rest(sign, functools.partial(behind, sign))
     store(decayed, decayed_out)
 
     def mate_arrives(s):
@@ -377,25 +381,31 @@
             device_id_type=MESH,
         )
 
-    def member_copy(i):
-        return pltpu.make_async_remote_copy(
-            src_ref=gath.at[chip, tpos],
-            dst_ref=gath.at[chip, tpos],
-            send_sem=gm_send.at[i],
-            recv_sem=gm_recv.at[i],
-            device_id={"member": 2 * lax.rem(chip + i, chips) + core},
-            device_id_type=MESH,
-        )
-
-    def column_copy(d):
-        return pltpu.make_async_remote_copy(
-            src_ref=gath.at[:, tpos],
-            dst_ref=gath.at[:, tpos],
-            send_sem=gt_send.at[d],
-            recv_sem=gt_recv.at[d],
-            device_id={"tower": lax.rem(tpos + d, nt)},
-            device_id_type=MESH,
-        )
+    def member_copies(i):
+        return [
+            pltpu.make_async_remote_copy(
+                src_ref=ref.at[chip, tpos],
+                dst_ref=ref.at[chip, tpos],
+                send_sem=gm_send.at[k, i],
+                recv_sem=gm_recv.at[k, i],
+                device_id={"member": 2 * lax.rem(chip + i, chips) + core},
+                device_id_type=MESH,
+            )
+            for k, ref in enumerate((errs, gath))
+        ]
+
+    def column_copies(d):
+        return [
+            pltpu.make_async_remote_copy(
+                src_ref=ref.at[:, tpos],
+                dst_ref=ref.at[:, tpos],
+                send_sem=gt_send.at[k, d],
+                recv_sem=gt_recv.at[k, d],
+                device_id={"tower": lax.rem(tpos + d, nt)},
+                device_id_type=MESH,
+            )
+            for k, ref in enumerate((errs, gath))
+        ]
 
     for sign in (1, -1):
         pass_on(sign, 1, functools.partial(behind, sign))
@@ -434,10 +444,13 @@
     clicks = jnp.where(seat == wanted, label_ref[...].astype(F32), 0.0)
     error = sigmoid(logit) - jnp.sum(clicks, axis=1, keepdims=True)
     gath[chip, tpos, :, :rank] = error * projected
-    gath[chip, tpos, :, rank : 2 * rank] = error * scaled
-    gath[chip, tpos, :, 2 * rank :] = error
+    gath[chip, tpos, :, rank:] = error * scaled
+    seat = lax.broadcasted_iota(jnp.int32, (piece, rank), 1)
+    wanted = lax.broadcasted_iota(jnp.int32, (piece, rank), 0)
+    errs[chip, tpos] = jnp.sum(jnp.where(seat == wanted, error, 0.0), axis=0, keepdims=True)
     for i in order:
-        member_copy(i).start()
+        for copy in member_copies(i):
+            copy.start()
     store(logits, logits_out)
 
     def far(sign, d, wanted):
@@ -451,9 +464,11 @@
     for i in order:
         tout_copy(i).start()
     for i in order:
-        member_copy(i).wait_recv()
+        for copy in member_copies(i):
+            copy.wait_recv()
     for d in range(1, nt):
-        column_copy(d).start()
+        for copy in column_copies(d):
+            copy.start()
     for d in range(2, chips):
         for sign in (1, -1):
             far(sign, d, jnp.logical_not(goes_on(sign)))
@@ -481,7 +496,8 @@
     for i in order:
         tout_copy(i).wait_recv()
     for d in range(1, nt):
-        column_copy(d).wait_recv()
+        for copy in column_copies(d):
+            copy.wait_recv()
 
     def back_copy(slot, source, target):
         return pltpu.make_async_remote_copy(
@@ -512,16 +528,27 @@
         else:
             ref[index] += value
 
+    errors = jnp.concatenate(
+        [
+            jnp.broadcast_to(errs[c, t], (piece, rank))
+            for c in range(chips)
+            for t in range(nt)
+        ],
+        axis=0,
+    )
+    seat = lax.broadcasted_iota(jnp.int32, (half, rank), 1)
+    wanted = lax.rem(lax.broadcasted_iota(jnp.int32, (half, rank), 0), piece)
+    errors = jnp.sum(jnp.where(seat == wanted, errors, 0.0), axis=1, keepdims=True)
     pair_rows = pl.ds(pl.multiple_of(chip * 2 * width, 2 * width), 2 * width)
     for t in range(towers):
         part = slice(t * outs, (t + 1) * outs)
         for c in range(half // chunk):
             span = slice(c * chunk, (c + 1) * chunk)
             here = slice(c * (chunk // own), (c + 1) * (chunk // own))
-            block = gath[here].reshape(chunk, 3 * rank)
+            block = gath[here].reshape(chunk, 2 * rank)
             go = split(
-                block[:, 2 * rank : 2 * rank + 1] * head[:, part]
-                + deep3(split(block[:, : 2 * rank]), (mixh[:, part], mixl[:, part]))
+                errors[span] * head[:, part]
+                + deep3(split(block), (mixh[:, part], mixl[:, part]))
             )
             grad_pooled = jnp.zeros((2 * width, chunk), F32)
             for k in range(hid // tile):
@@ -538,8 +565,8 @@
             copy.start()
 
     outputs = jnp.concatenate([tout_recv[c] for c in range(chips)], axis=0)
-    block = gath[...].reshape(half, 3 * rank)
-    value = deep3(split(outputs.T), split(block[:, : 2 * rank]))
+    block = gath[...].reshape(half, 2 * rank)
+    value = deep3(split(outputs.T), split(block))
     seat = lax.broadcasted_iota(jnp.int32, (pair_flat, flat), 1)
     wanted = lax.broadcasted_iota(jnp.int32, (pair_flat, flat), 0) + chip * pair_flat
     weights = jnp.sum(jnp.where(seat == wanted, head, 0.0), axis=1, keepdims=True)
@@ -584,10 +611,12 @@
         mate_copy(s).wait_send()
     for i in order:
         tout_copy(i).wait_send()
-        member_copy(i).wait_send()
+        for copy in member_copies(i):
+            copy.wait_send()
     for d in range(1, nt):
         tower_copy(d).wait_send()
-        column_copy(d).wait_send()
+        for copy in column_copies(d):
+            copy.wait_send()
     for t in range(towers):
         for copy in back_copies(t):
             copy.wait_send()
@@ -680,7 +709,8 @@
             pltpu.VMEM((chips, own, pair_flat), F32),
             pltpu.VMEM((own, 3 * rank), F32),
             pltpu.VMEM((nt, piece, 3 * rank), F32),
-            pltpu.VMEM((chips, nt, piece, 3 * rank), F32),
+            pltpu.VMEM((chips, nt, piece, 2 * rank), F32),
+            pltpu.VMEM((chips, nt, 1, rank), F32),
             pltpu.VMEM((half, hid), F32),
             pltpu.VMEM((towers, 2 * block_hid, half), BF16),
             pltpu.VMEM((towers, 2 * block_hid, half), BF16),
@@ -706,10 +736,10 @@
             sem((nt,)),
             sem((chips,)),
             sem((chips,)),
-            sem((chips,)),
-            sem((chips,)),
-            sem((nt,)),
-            sem((nt,)),
+            sem((2, chips)),
+            sem((2, chips)),
+            sem((2, nt)),
+            sem((2, nt)),
             sem((3 * towers + 1,)),
             sem((3 * towers + 1,)),
         ],

time: 47.8 us -> 41.4 us (0.87)
  Pallas kernels: 47 us -> 40.6 us
    pallas_call x1, Pallas kernels: 44.6 us -> 38.2 us  [per_device(): pl.pallas_call(functools.partial(main_kernel, (n, nt)), out_shape=(shape(...]
where the time goes in v3:
time: 41.4 us; the launch traced here: 41.3 us
  Pallas kernels  40.6 us (98%)
  between operations  0.64 us (2%)
    pallas_call x1, Pallas kernels, per_device(): pl.pallas_call(functools.partial(main_kernel, (n, nt)), out_shape=(shape(...  38.2 us
    pallas_call x1, Pallas kernels, per_device(): pl.pallas_call(final_kernel, out_shape=(shape((towers, width, rows), F32)...  2.4 us

profile of v3, /device:TPU:1, one launch (start us, length us, event | category | flops | bytes accessed | tf_op | source)
XLA Modules:
  0.0 41.3 jit_solution(7407108134221473032)
XLA Ops:
  0.6 38.2 %shard_map.162 = (f32[16,128]{1,0:T(8,128)}, f32[2,64,512]{2,1,0:T(8,128)}, f32[2,64,512]{2,1,0:T(8,128)}, f32[2,64,1024]{2,1,0:T(8,128)}, f32[2,128,256]{2,1,0:T(8,128)}, /*index=5*/f32[64,256]{1,0:T(8,128)}) custom-call(s32[2,4,512]{2,1,0:T(4,128)} %bitcast.11, s32[2,1,128]{2,1,0:T(1,128)} %touch_ref.1, s32[2,1,128]{2,1,0:T(1,128)} %elapsed_ref.1, ...), custom_call_target="tpu_custom_call" | custom-call | tf_op jit(solution)/shard_map/pallas_call | solution.py:680
  38.9 2.4 %shard_map.163 = (f32[2,64,512]{2,1,0:T(8,128)}, f32[2,1,512]{2,1,0:T(1,128)}, f32[64,2,1024]{2,1,0:T(2,128)}, f32[128,2,256]{2,1,0:T(2,128)}, f32[64,128]{1,0:T...) custom-call(f32[16,128]{1,0:T(8,128)} %get-tuple-element.20.logits_ref, f32[2,64,512]{2,1,0:T(8,128)} %get-tuple-element.21.decayed_ref, ...), custom_call_target="tpu_custom_call" | custom-call | tf_op jit(solution)/shard_map/pallas_call | solution.py:761

commit v4 on v3

--- a/solution.py
+++ b/solution.py
@@ -84,6 +84,8 @@
     tout_recv,
     stats,
     rs_buf,
+    line,
+    line_buf,
     gath,
     errs,
     act,
@@ -103,7 +105,7 @@
     logits,
     load_sem,
     store_sem,
-    own_send,
+    crit_send,
     mate_send,
     ag_send,
     ag_recv,
@@ -189,83 +191,83 @@
         value = tables_ref[t] * jnp.where(chosen > 0.0, chosen, 1.0)
         decayed[t] = value
         pairs.append(jnp.concatenate(split(value), axis=0))
-    def own_copy(sign, k, s):
+    out = jnp.where(chip < chips // 2, -1, 1)
+    inward = -out
+
+    def way(sign):
+        return jnp.where(sign > 0, 0, 1)
+
+    def slice_from(sign, j):
+        return lax.rem(chip + chips + sign * j, chips)
+
+    def own_copy(there, k, s, semaphore):
         at = slice_at(s)
         return pltpu.make_async_remote_copy(
             src_ref=pool.at[k, at],
             dst_ref=feats.at[me, at],
-            send_sem=own_send.at[(1 - sign) // 2, k, s],
-            recv_sem=ag_recv.at[me, s],
-            device_id={"member": 2 * (chip + sign) + k},
+            send_sem=semaphore,
+            recv_sem=ag_recv.at[chip, s],
+            device_id={"member": 2 * there + k},
             device_id_type=MESH,
         )
 
-    def mate_copy(s):
-        at = slice_at(s)
+    def mate_copy():
         return pltpu.make_async_remote_copy(
-            src_ref=pool.at[1 - core, at],
-            dst_ref=feats.at[me, at],
-            send_sem=mate_send.at[s],
-            recv_sem=ag_recv.at[me, s],
+            src_ref=pool.at[1 - core],
+            dst_ref=feats.at[me],
+            send_sem=mate_send.at[0],
+            recv_sem=ag_recv.at[chip, 0],
             device_id={"member": mate},
             device_id_type=MESH,
         )
 
-    def block_copy(sign, block, s):
-        at = slice_at(s)
+    def pair_copy(sign, d, s):
+        source, at = chip - sign * d, slice_at(s)
+        pair = pl.ds(2 * source, 2)
         return pltpu.make_async_remote_copy(
-            src_ref=feats.at[block, at],
-            dst_ref=feats.at[block, at],
-            send_sem=ag_send.at[(1 - sign) // 2, block, s],
-            recv_sem=ag_recv.at[block, s],
+            src_ref=feats.at[pair, at],
+            dst_ref=feats.at[pair, at],
+            send_sem=ag_send.at[way(sign), d],
+            recv_sem=ag_recv.at[source, s],
             device_id={"member": 2 * (chip + sign) + core},
             device_id_type=MESH,
         )
 
     def goes_on(sign):
-        return chip < chips - 1 if sign > 0 else chip > 0
+        return (chip + sign >= 0) & (chip + sign < chips)
 
     def present(sign, d):
-        return chip >= d if sign > 0 else chip + d < chips
-
-    def ahead(sign, act_on):
-        @pl.loop(0, chips - 1 - chip if sign > 0 else chip)
-        def _(i):
-            act_on(chips - 1 - i if sign > 0 else i)
-
-    def behind(sign, act_on):
-        @pl.loop(0, chip if sign > 0 else chips - 1 - chip)
-        def _(i):
-            act_on(chip - 1 - i if sign > 0 else chip + 1 + i)
-
-    def pass_on(sign, d, over):
-        def one(s):
-            for k in range(2):
-                block = 2 * (chip - sign * d) + k
-                block_copy(sign, block, s).wait_recv()
-
-                @pl.when(goes_on(sign))
-                def _():
-                    block_copy(sign, block, s).start()
-
-        @pl.when(present(sign, d))
+        return (chip - sign * d >= 0) & (chip - sign * d < chips)
+
+    def own_rest(sign):
+        @pl.when(goes_on(sign))
         def _():
-            over(one)
-
-    def at_once(sign):
-        if sign > 0:
-            return jnp.logical_or(chip == 0, chip == chips - 2)
-        return jnp.logical_or(chip == chips - 1, chip == 1)
-
-    def own_rest(sign):
-        def one(s):
-            for k in range(2):
-                own_copy(sign, k, s).start()
-
-        @pl.when(goes_on(sign) & jnp.logical_not(at_once(sign)))
+            for j in (0, *range(chips - 1, 1, -1)):
+                for k in range(2):
+                    own_copy(chip + sign, k, slice_from(sign, j), ag_send.at[way(sign), 0]).start()
+
+    def own_arrives(d):
+        for sign in (1, -1):
+
+            @pl.when(present(sign, d))
+            def _():
+                pair_copy(sign, d, chip).wait_recv()
+
+    def pass_on(part, sign, d):
+        @pl.when(goes_on(sign))
         def _():
-            one(chip)
-            behind(sign, one)
+            for j in part:
+                copy = pair_copy(sign, d, slice_from(sign, j))
+                if j:
+                    copy.wait_recv()
+                if j != 1:
+                    copy.start()
+
+    def arrives(sign, d):
+        @pl.when(jnp.logical_not(goes_on(sign)))
+        def _():
+            for j in range(chips - 1, 0, -1):
+                pair_copy(sign, d, slice_from(sign, j)).wait_recv()
 
     order = sorted(range(1, chips), key=lambda i: -min(i, chips - i))
     place = lax.broadcasted_iota(jnp.int32, (2 * own, rows), 1).astype(F32)
@@ -289,17 +291,11 @@
         if i == 1:
             pl.semaphore_wait(barrier, n - 1 + nt - 1)
 
-        @pl.when(jnp.logical_or(there > chip, at_once(1)) & goes_on(1))
-        def _():
+        if i < chips:
             for k in range(2):
-                own_copy(1, k, there).start()
-
-        @pl.when(jnp.logical_or(there < chip, at_once(-1)) & goes_on(-1))
-        def _():
-            for k in range(2):
-                own_copy(-1, k, there).start()
-
-        mate_copy(there).start()
+                own_copy(there, k, there, crit_send.at[0]).start()
+    own_rest(out)
+    mate_copy().start()
     feats[me] = pool[core]
 
     for copy in loads[:towers]:
@@ -311,11 +307,7 @@
             span = pl.ds(pl.multiple_of(i * 64, 64), 64)
             w1h[t, span, :], w1l[t, span, :] = split(stage[t, span, :])
 
-    for sign in (1, -1):
-        pass_on(sign, 1, functools.partial(ahead, sign))
-    for sign in (1, -1):
-        own_rest(sign)
-
+    own_rest(inward)
     for copy in loads[towers:]:
         copy.wait()
     for t in range(towers):
@@ -327,19 +319,18 @@
 
     head = head_ref[:, pl.ds(pl.multiple_of(tpos * flat, flat), flat)]
     mixh[...], mixl[...] = split(jnp.concatenate([lift[...].T * head, press[...].T], axis=0))
-
-    for d in range(2, chips):
-        for sign in (1, -1):
-            pass_on(sign, d, functools.partial(ahead, sign))
     store(decayed, decayed_out)
 
-    def mate_arrives(s):
-        block_copy(1, mate, s).wait_recv()
-
-    mate_arrives(chip)
+    def along(d, act_on):
+        for sign in (out, inward):
+            pl.when(present(sign, d))(functools.partial(act_on, sign, d))
+
+    mate_copy().wait_recv()
     for d in range(1, chips):
-        for sign in (1, -1):
-            pass_on(sign, d, lambda act_on: act_on(chip))
+        own_arrives(d)
+    for d in range(1, chips):
+        along(d, functools.partial(pass_on, [0]))
+    along(1, functools.partial(pass_on, [chips - 1]))
     flat_out = []
     for t in range(towers):
         part = slice(t * width, (t + 1) * width)
@@ -347,24 +338,31 @@
         h = few3(split(x), (w1h[t], w1l[t]))
         flat_out.append(few3(split(h * sigmoid(h)), (w2h[t], w2l[t])))
     flat_out = jnp.concatenate(flat_out, axis=1)
-    stats[:, : 2 * rank] = few3(split(flat_out), (mixh[...], mixl[...]), NT)
-    stats[:, 2 * rank :] = jnp.broadcast_to(
-        jnp.sum(flat_out * head, axis=1, keepdims=True), (own, rank)
-    )
-
-    def tower_copy(d):
+    stats[...] = few3(split(flat_out), (mixh[...], mixl[...]), NT).reshape(nt, piece, 2 * rank)
+    linear = jnp.sum(flat_out * head, axis=1, keepdims=True)
+    seat = lax.broadcasted_iota(jnp.int32, (piece, rank), 1)
+    wanted = lax.broadcasted_iota(jnp.int32, (piece, rank), 0)
+    for k in range(nt):
+        row = jnp.where(seat == wanted, linear[k * piece : (k + 1) * piece], 0.0)
+        line[k] = jnp.sum(row, axis=0, keepdims=True)
+
+    def tower_copies(d):
         other = lax.rem(tpos + d, nt)
-        return pltpu.make_async_remote_copy(
-            src_ref=stats.at[pl.ds(pl.multiple_of(other * piece, piece), piece)],
-            dst_ref=rs_buf.at[tpos],
-            send_sem=rs_send.at[d],
-            recv_sem=rs_recv.at[d],
-            device_id={"tower": other},
-            device_id_type=MESH,
-        )
+        return [
+            pltpu.make_async_remote_copy(
+                src_ref=ref.at[other],
+                dst_ref=buf.at[tpos],
+                send_sem=rs_send.at[k],
+                recv_sem=rs_recv.at[k, d - 1],
+                device_id={"tower": other},
+                device_id_type=MESH,
+            )
+            for k, (ref, buf) in enumerate(((line, line_buf), (stats, rs_buf)))
+        ]
 
     for d in range(1, nt):
-        tower_copy(d).start()
+        for copy in tower_copies(d):
+            copy.start()
 
     for c in range(chips):
         tout_send[c] = flat_out[:, c * pair_flat : (c + 1) * pair_flat]
@@ -375,42 +373,46 @@
         return pltpu.make_async_remote_copy(
             src_ref=tout_send.at[there],
             dst_ref=tout_recv.at[chip],
-            send_sem=to_send.at[i],
-            recv_sem=to_recv.at[i],
+            send_sem=to_send.at[0],
+            recv_sem=to_recv.at[i - 1],
             device_id={"member": 2 * there + core},
             device_id_type=MESH,
         )
 
-    def member_copies(i):
+    def member_copies(i, there):
         return [
             pltpu.make_async_remote_copy(
                 src_ref=ref.at[chip, tpos],
                 dst_ref=ref.at[chip, tpos],
-                send_sem=gm_send.at[k, i],
-                recv_sem=gm_recv.at[k, i],
-                device_id={"member": 2 * lax.rem(chip + i, chips) + core},
+                send_sem=gm_send.at[k],
+                recv_sem=gm_recv.at[k, i - 1],
+                device_id={"member": 2 * there + core},
                 device_id_type=MESH,
             )
             for k, ref in enumerate((errs, gath))
         ]
 
-    def column_copies(d):
+    def column_copies(d, source, count):
+        where = pl.ds(source, count)
         return [
             pltpu.make_async_remote_copy(
-                src_ref=ref.at[:, tpos],
-                dst_ref=ref.at[:, tpos],
-                send_sem=gt_send.at[k, d],
-                recv_sem=gt_recv.at[k, d],
+                src_ref=ref.at[where, tpos],
+                dst_ref=ref.at[where, tpos],
+                send_sem=gt_send.at[k],
+                recv_sem=gt_recv.at[k, d - 1],
                 device_id={"tower": lax.rem(tpos + d, nt)},
                 device_id_type=MESH,
             )
             for k, ref in enumerate((errs, gath))
         ]
 
-    for sign in (1, -1):
-        pass_on(sign, 1, functools.partial(behind, sign))
-    for sign in (1, -1):
-        behind(sign, mate_arrives)
+    def column_start(source):
+        for d in range(1, nt):
+            for copy in column_copies(d, source, 1):
+                copy.start()
+
+    along(1, functools.partial(pass_on, range(chips - 2, 0, -1)))
+    along(1, arrives)
     per = 4
     together = per * width
 
@@ -432,46 +434,46 @@
                 stage[t, span, lanes] = value
 
     for d in range(1, nt):
-        tower_copy(d).wait_recv()
-    summed = stats[pl.ds(pl.multiple_of(tpos * piece, piece), piece), :]
+        for copy in tower_copies(d):
+            copy.wait_recv()
+    summed, linear = stats[tpos], line[tpos]
     for d in range(1, nt):
         summed = summed + rs_buf[lax.rem(tpos + d, nt)]
-    scaled, projected = summed[:, :rank], summed[:, rank : 2 * rank]
-    logit = jnp.sum(projected * scaled, axis=1, keepdims=True) + summed[:, 2 * rank :]
+        linear = linear + line_buf[lax.rem(tpos + d, nt)]
+    scaled, projected = summed[:, :rank], summed[:, rank:]
+    linear = jnp.sum(jnp.where(seat == wanted, linear, 0.0), axis=1, keepdims=True)
+    logit = jnp.sum(projected * scaled, axis=1, keepdims=True) + linear
+    logit = jnp.broadcast_to(logit, (piece, rank))
     logits[...] = logit
-    seat = lax.broadcasted_iota(jnp.int32, (piece, own), 1)
-    wanted = lax.broadcasted_iota(jnp.int32, (piece, own), 0) + tpos * piece
-    clicks = jnp.where(seat == wanted, label_ref[...].astype(F32), 0.0)
+    place = lax.broadcasted_iota(jnp.int32, (piece, own), 1)
+    mine = lax.broadcasted_iota(jnp.int32, (piece, own), 0) + tpos * piece
+    clicks = jnp.where(place == mine, label_ref[...].astype(F32), 0.0)
     error = sigmoid(logit) - jnp.sum(clicks, axis=1, keepdims=True)
     gath[chip, tpos, :, :rank] = error * projected
     gath[chip, tpos, :, rank:] = error * scaled
-    seat = lax.broadcasted_iota(jnp.int32, (piece, rank), 1)
-    wanted = lax.broadcasted_iota(jnp.int32, (piece, rank), 0)
     errs[chip, tpos] = jnp.sum(jnp.where(seat == wanted, error, 0.0), axis=0, keepdims=True)
     for i in order:
-        for copy in member_copies(i):
+        for copy in member_copies(i, lax.rem(chip + i, chips)):
             copy.start()
+    column_start(chip)
     store(logits, logits_out)
 
-    def far(sign, d, wanted):
-        @pl.when(wanted)
+    for d in range(2, chips):
+        along(d, functools.partial(pass_on, [chips - 1]))
+    for source in sorted(range(chips), key=lambda c: -min(c, chips - 1 - c)):
+
+        @pl.when(chip != source)
         def _():
-            pass_on(sign, d, functools.partial(behind, sign))
+            for copy in member_copies(lax.rem(chip + chips - source, chips), source):
+                copy.wait_recv()
+            column_start(source)
 
     for d in range(2, chips):
-        for sign in (1, -1):
-            far(sign, d, goes_on(sign))
+        along(d, functools.partial(pass_on, range(chips - 2, 0, -1)))
     for i in order:
         tout_copy(i).start()
-    for i in order:
-        for copy in member_copies(i):
-            copy.wait_recv()
-    for d in range(1, nt):
-        for copy in column_copies(d):
-            copy.start()
     for d in range(2, chips):
-        for sign in (1, -1):
-            far(sign, d, jnp.logical_not(goes_on(sign)))
+        along(d, arrives)
 
     start = pl.multiple_of(chip * pair_hid, pair_hid)
     groups = n // per
@@ -493,11 +495,40 @@
             pth[t, :, span], ptl[t, :, span] = split(both.T)
             acth[t, :, span], actl[t, :, span] = split(act[span, pl.ds(start, pair_hid)].T)
 
+    def sent(ref, semaphore):
+        pltpu.make_async_remote_copy(
+            src_ref=ref,
+            dst_ref=ref,
+            send_sem=semaphore,
+            recv_sem=ag_recv.at[0, 0],
+            device_id={"member": mate},
+            device_id_type=MESH,
+        ).wait_send()
+
+    sent(pool.at[0], mate_send.at[0])
+    for k, ref in enumerate((line, stats)):
+        sent(ref.at[: nt - 1], rs_send.at[k])
+    sent(feats.at[:2, : half - own], crit_send.at[0])
+    for sign in (1, -1):
+
+        @pl.when(goes_on(sign))
+        def _():
+            sent(pool.at[:, : half - own], ag_send.at[way(sign), 0])
+            for d in range(1, chips):
+
+                @pl.when(present(sign, d))
+                def _():
+                    sent(feats.at[:2, : half - own], ag_send.at[way(sign), d])
+
     for i in order:
         tout_copy(i).wait_recv()
     for d in range(1, nt):
-        for copy in column_copies(d):
+        for copy in column_copies(d, 0, chips):
             copy.wait_recv()
+    sent(tout_send.at[: chips - 1], to_send.at[0])
+    for k, ref in enumerate((errs, gath)):
+        sent(ref.at[: chips - 1, 0], gm_send.at[k])
+        sent(ref.at[:, : nt - 1], gt_send.at[k])
 
     def back_copy(slot, source, target):
         return pltpu.make_async_remote_copy(
@@ -593,30 +624,6 @@
     glp_in[...] += glp[rows_of(core, pair_flat // 2), :]
     store(glp_in, glp_out)
 
-    for sign in (1, -1):
-
-        @pl.when(goes_on(sign))
-        def _():
-            for s in range(chips):
-                for k in range(2):
-                    own_copy(sign, k, s).wait_send()
-                for d in range(1, chips):
-
-                    @pl.when(present(sign, d))
-                    def _():
-                        for k in range(2):
-                            block_copy(sign, 2 * (chip - sign * d) + k, s).wait_send()
-
-    for s in range(chips):
-        mate_copy(s).wait_send()
-    for i in order:
-        tout_copy(i).wait_send()
-        for copy in member_copies(i):
-            copy.wait_send()
-    for d in range(1, nt):
-        tower_copy(d).wait_send()
-        for copy in column_copies(d):
-            copy.wait_send()
     for t in range(towers):
         for copy in back_copies(t):
             copy.wait_send()
@@ -707,8 +714,10 @@
             pltpu.VMEM((n, half, lanes), F32),
             pltpu.VMEM((chips, own, pair_flat), F32),
             pltpu.VMEM((chips, own, pair_flat), F32),
-            pltpu.VMEM((own, 3 * rank), F32),
-            pltpu.VMEM((nt, piece, 3 * rank), F32),
+            pltpu.VMEM((nt, piece, 2 * rank), F32),
+            pltpu.VMEM((nt, piece, 2 * rank), F32),
+            pltpu.VMEM((nt, 1, rank), F32),
+            pltpu.VMEM((nt, 1, rank), F32),
             pltpu.VMEM((chips, nt, piece, 2 * rank), F32),
             pltpu.VMEM((chips, nt, 1, rank), F32),
             pltpu.VMEM((half, hid), F32),
@@ -728,18 +737,18 @@
             pltpu.VMEM((piece, rank), F32),
             sem((2 * towers + 2,)),
             sem((3 + 3 * towers,)),
-            sem((2, 2, chips)),
-            sem((chips,)),
-            sem((2, n, chips)),
-            sem((n, chips)),
-            sem((nt,)),
-            sem((nt,)),
-            sem((chips,)),
-            sem((chips,)),
+            sem((1,)),
+            sem((1,)),
             sem((2, chips)),
-            sem((2, chips)),
-            sem((2, nt)),
-            sem((2, nt)),
+            sem((chips, chips)),
+            sem((2,)),
+            sem((2, nt - 1)),
+            sem((1,)),
+            sem((chips - 1,)),
+            sem((2,)),
+            sem((2, chips - 1)),
+            sem((2,)),
+            sem((2, nt - 1)),
             sem((3 * towers + 1,)),
             sem((3 * towers + 1,)),
         ],

time: 41.4 us -> 40.2 us (0.971)
  Pallas kernels: 40.6 us -> 39.4 us
    pallas_call x1, Pallas kernels: 38.2 us -> 37 us  [per_device(): pl.pallas_call(functools.partial(main_kernel, (n, nt)), out_shape=(shape(...]
where the time goes in v4:
time: 40.2 us; the launch traced here: 40.1 us
  Pallas kernels  39.4 us (98%)
  between operations  0.64 us (2%)
    pallas_call x1, Pallas kernels, per_device(): pl.pallas_call(functools.partial(main_kernel, (n, nt)), out_shape=(shape(...  37 us
    pallas_call x1, Pallas kernels, per_device(): pl.pallas_call(final_kernel, out_shape=(shape((towers, width, rows), F32)...  2.4 us

profile of v4, /device:TPU:1, one launch (start us, length us, event | category | flops | bytes accessed | tf_op | source)
XLA Modules:
  0.0 40.1 jit_solution(11431908615285865334)
XLA Ops:
  0.6 37.0 %shard_map.162 = (f32[16,128]{1,0:T(8,128)}, f32[2,64,512]{2,1,0:T(8,128)}, f32[2,64,512]{2,1,0:T(8,128)}, f32[2,64,1024]{2,1,0:T(8,128)}, f32[2,128,256]{2,1,0:T(8,128)}, /*index=5*/f32[64,256]{1,0:T(8,128)}) custom-call(s32[2,4,512]{2,1,0:T(4,128)} %bitcast.11, s32[2,1,128]{2,1,0:T(1,128)} %touch_ref.1, s32[2,1,128]{2,1,0:T(1,128)} %elapsed_ref.1, ...), custom_call_target="tpu_custom_call" | custom-call | tf_op jit(solution)/shard_map/pallas_call | solution.py:687
  37.7 2.4 %shard_map.163 = (f32[2,64,512]{2,1,0:T(8,128)}, f32[2,1,512]{2,1,0:T(1,128)}, f32[64,2,1024]{2,1,0:T(2,128)}, f32[128,2,256]{2,1,0:T(2,128)}, f32[64,128]{1,0:T...) custom-call(f32[16,128]{1,0:T(8,128)} %get-tuple-element.20.logits_ref, f32[2,64,512]{2,1,0:T(8,128)} %get-tuple-element.21.decayed_ref, ...), custom_call_target="tpu_custom_call" | custom-call | tf_op jit(solution)/shard_map/pallas_call | solution.py:770

commit v5 on v4

--- a/solution.py
+++ b/solution.py
@@ -108,6 +108,7 @@
     crit_send,
     mate_send,
     ag_send,
+    relay_send,
     ag_recv,
     rs_send,
     rs_recv,
@@ -192,13 +193,7 @@
         decayed[t] = value
         pairs.append(jnp.concatenate(split(value), axis=0))
     out = jnp.where(chip < chips // 2, -1, 1)
-    inward = -out
-
-    def way(sign):
-        return jnp.where(sign > 0, 0, 1)
-
-    def slice_from(sign, j):
-        return lax.rem(chip + chips + sign * j, chips)
+    near_end = (chip == 1) | (chip == chips - 2)
 
     def own_copy(there, k, s, semaphore):
         at = slice_at(s)
@@ -221,60 +216,73 @@
             device_id_type=MESH,
         )
 
-    def pair_copy(sign, d, s):
-        source, at = chip - sign * d, slice_at(s)
-        pair = pl.ds(2 * source, 2)
+    def pair_copy(source, s, semaphore):
+        pair, at = pl.ds(2 * source, 2), slice_at(s)
         return pltpu.make_async_remote_copy(
             src_ref=feats.at[pair, at],
             dst_ref=feats.at[pair, at],
-            send_sem=ag_send.at[way(sign), d],
+            send_sem=semaphore,
             recv_sem=ag_recv.at[source, s],
-            device_id={"member": 2 * (chip + sign) + core},
+            device_id={"member": 2 * lax.rem(chip + out + chips, chips) + core},
             device_id_type=MESH,
         )
 
-    def goes_on(sign):
-        return (chip + sign >= 0) & (chip + sign < chips)
-
-    def present(sign, d):
-        return (chip - sign * d >= 0) & (chip - sign * d < chips)
-
-    def own_rest(sign):
-        @pl.when(goes_on(sign))
+    def slice_from(there, sign, j):
+        return lax.rem(there + chips + sign * j, chips)
+
+    def whole_copies(there, semaphore):
+        towards = jnp.where(there < chips // 2, -1, 1)
+        return [
+            own_copy(there, k, slice_from(there, towards, j), semaphore)
+            for j in range(chips - 1, 0, -1)
+            for k in range(2)
+        ]
+
+    def end_each(act_on):
+        @pl.when(near_end)
         def _():
-            for j in (0, *range(chips - 1, 1, -1)):
-                for k in range(2):
-                    own_copy(chip + sign, k, slice_from(sign, j), ag_send.at[way(sign), 0]).start()
-
-    def own_arrives(d):
-        for sign in (1, -1):
-
-            @pl.when(present(sign, d))
-            def _():
-                pair_copy(sign, d, chip).wait_recv()
-
-    def pass_on(part, sign, d):
-        @pl.when(goes_on(sign))
+            act_on(chip + out, ag_send.at[0, 0])
+
+    def inner_each(hops, act_on):
+        for sign in (-1, 1):
+            for i in hops:
+                there = chip + sign * out * i
+
+                @pl.when((there > 0) & (there < chips - 1))
+                def _():
+                    act_on(there, ag_send.at[(1 + sign) // 2, i])
+
+    def start_all(there, semaphore):
+        for copy in whole_copies(there, semaphore):
+            copy.start()
+
+    def own_arrives(i):
+        pair_copy(lax.rem(chip + i, chips), chip, relay_send.at[0]).wait_recv()
+
+    def relay(d, part):
+        @pl.when(near_end)
         def _():
             for j in part:
-                copy = pair_copy(sign, d, slice_from(sign, j))
+                copy = pair_copy(chip - out * d, slice_from(chip, out, j), relay_send.at[d - 1])
                 if j:
                     copy.wait_recv()
-                if j != 1:
-                    copy.start()
-
-    def arrives(sign, d):
-        @pl.when(jnp.logical_not(goes_on(sign)))
+                copy.start()
+
+    def rest_arrives(i):
+        source = lax.rem(chip + i, chips)
+        pair_copy(source, slice_from(chip, out, 1), relay_send.at[0]).wait_recv()
+
+        @pl.when(jnp.logical_not(near_end) | (source == chip + out))
         def _():
-            for j in range(chips - 1, 0, -1):
-                pair_copy(sign, d, slice_from(sign, j)).wait_recv()
+            for j in range(2, chips):
+                pair_copy(source, slice_from(chip, out, j), relay_send.at[0]).wait_recv()
 
     order = sorted(range(1, chips), key=lambda i: -min(i, chips - i))
     place = lax.broadcasted_iota(jnp.int32, (2 * own, rows), 1).astype(F32)
-    for i in range(1, chips + 1):
-        there = lax.rem(jnp.where(chip < chips // 2, chip + chips - i, chip + i), chips)
+
+    def count(there):
         span = pl.ds(pl.multiple_of(there * 2 * own, 2 * own), 2 * own)
-        pooled = []
+        found = []
         for t in range(towers):
             counts = jnp.zeros((2 * own, rows), F32)
             for b in range(bags):
@@ -283,18 +291,32 @@
             counts = counts.astype(BF16)
             for k in range(2):
                 counts_ref[t, k, slice_at(there), :] = counts[k * own : (k + 1) * own]
-            both = dot1(counts, pairs[t], NT)
-            pooled.append(both[:, :width] + both[:, width:])
-        pooled = jnp.concatenate(pooled, axis=1)
+            found.append(counts)
+        return found
+
+    mirrored = jnp.where(chip < chips // 2, chip, chips - 1 - chip)
+    stops = [chips // 2 + i for i in range(chips // 2)]
+    stops += [lax.rem(mirrored + i, chips // 2) for i in range(1, chips // 2 + 1)]
+    stops = [jnp.where(chip < chips // 2, stop, chips - 1 - stop) for stop in stops]
+    found = count(stops[0])
+    for i, there in enumerate(stops):
+        both = [dot1(counts, pairs[t], NT) for t, counts in enumerate(found)]
+        if i + 1 < chips:
+            found = count(stops[i + 1])
+        pooled = jnp.concatenate([x[:, :width] + x[:, width:] for x in both], axis=1)
         for k in range(2):
             pool[k, slice_at(there), :] = pooled[k * own : (k + 1) * own]
-        if i == 1:
+        if i == 0:
             pl.semaphore_wait(barrier, n - 1 + nt - 1)
-
-        if i < chips:
+        if i + 1 < chips:
             for k in range(2):
                 own_copy(there, k, there, crit_send.at[0]).start()
-    own_rest(out)
+
+        @pl.when(near_end & (there != chip + out))
+        def _():
+            for k in range(2):
+                own_copy(chip + out, k, there, ag_send.at[0, 0]).start()
+
     mate_copy().start()
     feats[me] = pool[core]
 
@@ -307,7 +329,7 @@
             span = pl.ds(pl.multiple_of(i * 64, 64), 64)
             w1h[t, span, :], w1l[t, span, :] = split(stage[t, span, :])
 
-    own_rest(inward)
+    inner_each([1], start_all)
     for copy in loads[towers:]:
         copy.wait()
     for t in range(towers):
@@ -321,16 +343,12 @@
     mixh[...], mixl[...] = split(jnp.concatenate([lift[...].T * head, press[...].T], axis=0))
     store(decayed, decayed_out)
 
-    def along(d, act_on):
-        for sign in (out, inward):
-            pl.when(present(sign, d))(functools.partial(act_on, sign, d))
-
     mate_copy().wait_recv()
-    for d in range(1, chips):
-        own_arrives(d)
-    for d in range(1, chips):
-        along(d, functools.partial(pass_on, [0]))
-    along(1, functools.partial(pass_on, [chips - 1]))
+    for i in range(1, chips):
+        own_arrives(i)
+    inner_each(range(2, chips - 1), start_all)
+    for d in range(1, chips - 1):
+        relay(d, [0])
     flat_out = []
     for t in range(towers):
         part = slice(t * width, (t + 1) * width)
@@ -411,8 +429,9 @@
             for copy in column_copies(d, source, 1):
                 copy.start()
 
-    along(1, functools.partial(pass_on, range(chips - 2, 0, -1)))
-    along(1, arrives)
+    relay(1, range(chips - 1, 1, -1))
+    beside = 1 - 2 * lax.rem(chip, 2)
+    rest_arrives(beside + chips)
     per = 4
     together = per * width
 
@@ -458,8 +477,8 @@
     column_start(chip)
     store(logits, logits_out)
 
-    for d in range(2, chips):
-        along(d, functools.partial(pass_on, [chips - 1]))
+    for d in range(2, chips - 1):
+        relay(d, range(chips - 1, 1, -1))
     for source in sorted(range(chips), key=lambda c: -min(c, chips - 1 - c)):
 
         @pl.when(chip != source)
@@ -468,12 +487,8 @@
                 copy.wait_recv()
             column_start(source)
 
-    for d in range(2, chips):
-        along(d, functools.partial(pass_on, range(chips - 2, 0, -1)))
-    for i in order:
-        tout_copy(i).start()
-    for d in range(2, chips):
-        along(d, arrives)
+    for i in range(1, chips):
+        pl.when(lax.rem(chip + i, chips) != chip + beside)(functools.partial(rest_arrives, i))
 
     start = pl.multiple_of(chip * pair_hid, pair_hid)
     groups = n // per
@@ -509,23 +524,22 @@
     for k, ref in enumerate((line, stats)):
         sent(ref.at[: nt - 1], rs_send.at[k])
     sent(feats.at[:2, : half - own], crit_send.at[0])
-    for sign in (1, -1):
-
-        @pl.when(goes_on(sign))
-        def _():
-            sent(pool.at[:, : half - own], ag_send.at[way(sign), 0])
-            for d in range(1, chips):
-
-                @pl.when(present(sign, d))
-                def _():
-                    sent(feats.at[:2, : half - own], ag_send.at[way(sign), d])
+    def sent_all(there, semaphore):
+        sent(pool.at[:, : half - own], semaphore)
+
+    end_each(sent_all)
+    inner_each(range(1, chips - 1), sent_all)
+
+    @pl.when(near_end)
+    def _():
+        for d in range(1, chips - 1):
+            sent(feats.at[:2, : half - own], relay_send.at[d - 1])
 
     for i in order:
-        tout_copy(i).wait_recv()
+        tout_copy(i).start()
     for d in range(1, nt):
         for copy in column_copies(d, 0, chips):
             copy.wait_recv()
-    sent(tout_send.at[: chips - 1], to_send.at[0])
     for k, ref in enumerate((errs, gath)):
         sent(ref.at[: chips - 1, 0], gm_send.at[k])
         sent(ref.at[:, : nt - 1], gt_send.at[k])
@@ -595,6 +609,9 @@
         for copy in back_copies(t):
             copy.start()
 
+    for i in order:
+        tout_copy(i).wait_recv()
+    sent(tout_send.at[: chips - 1], to_send.at[0])
     outputs = jnp.concatenate([tout_recv[c] for c in range(chips)], axis=0)
     block = gath[...].reshape(half, 2 * rank)
     value = deep3(split(outputs.T), split(block))
@@ -739,7 +756,8 @@
             sem((3 + 3 * towers,)),
             sem((1,)),
             sem((1,)),
-            sem((2, chips)),
+            sem((2, chips - 1)),
+            sem((chips - 2,)),
             sem((chips, chips)),
             sem((2,)),
             sem((2, nt - 1)),

time: 40.2 us -> 38.5 us (0.958)
  Pallas kernels: 39.4 us -> 37.7 us
    pallas_call x1, Pallas kernels: 37 us -> 35.3 us  [per_device(): pl.pallas_call(functools.partial(main_kernel, (n, nt)), out_shape=(shape(...]
where the time goes in v5:
time: 38.5 us; the launch traced here: 38.4 us
  Pallas kernels  37.7 us (98%)
  between operations  0.64 us (2%)
    pallas_call x1, Pallas kernels, per_device(): pl.pallas_call(functools.partial(main_kernel, (n, nt)), out_shape=(shape(...  35.3 us
    pallas_call x1, Pallas kernels, per_device(): pl.pallas_call(final_kernel, out_shape=(shape((towers, width, rows), F32)...  2.4 us

profile of v5, /device:TPU:1, one launch (start us, length us, event | category | flops | bytes accessed | tf_op | source)
XLA Modules:
  0.0 38.4 jit_solution(1764702725925834620)
XLA Ops:
  0.6 35.3 %shard_map.162 = (f32[16,128]{1,0:T(8,128)}, f32[2,64,512]{2,1,0:T(8,128)}, f32[2,64,512]{2,1,0:T(8,128)}, f32[2,64,1024]{2,1,0:T(8,128)}, f32[2,128,256]{2,1,0:T(8,128)}, /*index=5*/f32[64,256]{1,0:T(8,128)}) custom-call(s32[2,4,512]{2,1,0:T(4,128)} %bitcast.11, s32[2,1,128]{2,1,0:T(1,128)} %touch_ref.1, s32[2,1,128]{2,1,0:T(1,128)} %elapsed_ref.1, ...), custom_call_target="tpu_custom_call" | custom-call | tf_op jit(solution)/shard_map/pallas_call | solution.py:704
  36.0 2.4 %shard_map.163 = (f32[2,64,512]{2,1,0:T(8,128)}, f32[2,1,512]{2,1,0:T(1,128)}, f32[64,2,1024]{2,1,0:T(2,128)}, f32[128,2,256]{2,1,0:T(2,128)}, f32[64,128]{1,0:T...) custom-call(f32[16,128]{1,0:T(8,128)} %get-tuple-element.20.logits_ref, f32[2,64,512]{2,1,0:T(8,128)} %get-tuple-element.21.decayed_ref, ...), custom_call_target="tpu_custom_call" | custom-call | tf_op jit(solution)/shard_map/pallas_call | solution.py:788

commit v6 on v5

--- a/solution.py
+++ b/solution.py
@@ -77,7 +77,6 @@
     mixl,
     cols,
     counts_ref,
-    decayed,
     pool,
     feats,
     tout_send,
@@ -101,10 +100,7 @@
     gpool_in,
     glp,
     glp_in,
-    gt,
-    logits,
     load_sem,
-    store_sem,
     crit_send,
     mate_send,
     ag_send,
@@ -166,12 +162,6 @@
             barrier, inc=1, device_id={"tower": lax.rem(tpos + d, nt)}, device_id_type=MESH
         )
 
-    stores = []
-
-    def store(source, target):
-        stores.append(pltpu.make_async_copy(source, target, store_sem.at[len(stores)]))
-        stores[-1].start()
-
     def slice_at(index):
         return pl.ds(pl.multiple_of(index * own, own), own)
 
@@ -190,7 +180,7 @@
         ids, rates = owed[:, 2 * t : 2 * t + 1], owed[:, 2 * t + 1 : 2 * t + 2]
         chosen = jnp.sum(jnp.where(place == ids, rates, 0.0), axis=0, keepdims=True)
         value = tables_ref[t] * jnp.where(chosen > 0.0, chosen, 1.0)
-        decayed[t] = value
+        decayed_out[t] = value
         pairs.append(jnp.concatenate(split(value), axis=0))
     out = jnp.where(chip < chips // 2, -1, 1)
     near_end = (chip == 1) | (chip == chips - 2)
@@ -341,7 +331,6 @@
 
     head = head_ref[:, pl.ds(pl.multiple_of(tpos * flat, flat), flat)]
     mixh[...], mixl[...] = split(jnp.concatenate([lift[...].T * head, press[...].T], axis=0))
-    store(decayed, decayed_out)
 
     mate_copy().wait_recv()
     for i in range(1, chips):
@@ -463,7 +452,7 @@
     linear = jnp.sum(jnp.where(seat == wanted, linear, 0.0), axis=1, keepdims=True)
     logit = jnp.sum(projected * scaled, axis=1, keepdims=True) + linear
     logit = jnp.broadcast_to(logit, (piece, rank))
-    logits[...] = logit
+    logits_out[...] = logit
     place = lax.broadcasted_iota(jnp.int32, (piece, own), 1)
     mine = lax.broadcasted_iota(jnp.int32, (piece, own), 0) + tpos * piece
     clicks = jnp.where(place == mine, label_ref[...].astype(F32), 0.0)
@@ -475,7 +464,6 @@
         for copy in member_copies(i, lax.rem(chip + i, chips)):
             copy.start()
     column_start(chip)
-    store(logits, logits_out)
 
     for d in range(2, chips - 1):
         relay(d, range(chips - 1, 1, -1))
@@ -600,10 +588,10 @@
                 lanes = slice(k * tile, (k + 1) * tile)
                 grad_act = deep3(go, (w2h[t, lanes, :], w2l[t, lanes, :]), NT)
                 grad_hidden = split(grad_act * stage[t, span, lanes])
-                value = deep3((pth[t, :, span], ptl[t, :, span]), grad_hidden)
+                value = few3((pth[t, :, span], ptl[t, :, span]), grad_hidden)
                 put(gf, (t, slice(None), lanes), value, c == 0)
                 first = (w1h[t, pair_rows, lanes], w1l[t, pair_rows, lanes])
-                grad_pooled = grad_pooled + deep3(first, grad_hidden, NT)
+                grad_pooled = grad_pooled + few3(first, grad_hidden, NT)
             gpool[t, :, span] = grad_pooled
             put(gsec, (t,), deep3((acth[t, :, span], actl[t, :, span]), go), c == 0)
         for copy in back_copies(t):
@@ -629,24 +617,18 @@
         from_mate[0].wait_recv()
         theirs = jnp.concatenate(split(gpool_in[t]), axis=0)
         both = both + dot1(theirs, counts_ref[t, 1 - core])
-        gt[t] = both[:width] + both[width:]
-        store(gt.at[t], gt_out.at[t])
+        gt_out[t] = both[:width] + both[width:]
         from_mate[1].wait_recv()
-        gf_in[t] += gf[t, rows_of(core, width), :]
-        store(gf_in.at[t], gf_out.at[t])
+        gf_out[t] = gf_in[t] + gf[t, rows_of(core, width), :]
         from_mate[2].wait_recv()
-        gsec_in[t] += gsec[t, rows_of(core, block_hid), :]
-        store(gsec_in.at[t], gsec_out.at[t])
+        gsec_out[t] = gsec_in[t] + gsec[t, rows_of(core, block_hid), :]
     lift_copy().wait_recv()
-    glp_in[...] += glp[rows_of(core, pair_flat // 2), :]
-    store(glp_in, glp_out)
+    glp_out[...] = glp_in[...] + glp[rows_of(core, pair_flat // 2), :]
 
     for t in range(towers):
         for copy in back_copies(t):
             copy.wait_send()
     lift_copy().wait_send()
-    for copy in stores:
-        copy.wait()
 
 
 def final_kernel(
@@ -704,15 +686,15 @@
     between = pl.pallas_call(
         functools.partial(main_kernel, (n, nt)),
         out_shape=(
-            shape((piece, rank), F32),
-            shape((towers, width, rows), F32),
-            shape((towers, width, rows), F32),
-            shape((towers, width, hid), F32),
-            shape((towers, block_hid, outs), F32),
-            shape((pair_flat // 2, 2 * rank), F32),
+            pltpu.VMEM((piece, rank), F32),
+            pltpu.VMEM((towers, width, rows), F32),
+            pltpu.VMEM((towers, width, rows), F32),
+            pltpu.VMEM((towers, width, hid), F32),
+            pltpu.VMEM((towers, block_hid, outs), F32),
+            pltpu.VMEM((pair_flat // 2, 2 * rank), F32),
         ),
         in_specs=[vmem] * 4 + [anys] * 4 + [vmem] * 2,
-        out_specs=[anys] * 6,
+        out_specs=[vmem] * 6,
         scratch_shapes=[
             pltpu.VMEM((towers, max(half, fin), hid), F32),
             pltpu.VMEM((towers, fin, hid), BF16),
@@ -726,7 +708,6 @@
             pltpu.VMEM((2 * rank, flat), BF16),
             pltpu.VMEM((total, 128), F32),
             pltpu.VMEM((towers, 2, half, rows), BF16),
-            pltpu.VMEM((towers, width, rows), F32),
             pltpu.VMEM((2, half, lanes), F32),
             pltpu.VMEM((n, half, lanes), F32),
             pltpu.VMEM((chips, own, pair_flat), F32),
@@ -750,10 +731,7 @@
             pltpu.VMEM((towers, width, half), F32),
             pltpu.VMEM((pair_flat, 2 * rank), F32),
             pltpu.VMEM((pair_flat // 2, 2 * rank), F32),
-            pltpu.VMEM((towers, width, rows), F32),
-            pltpu.VMEM((piece, rank), F32),
             sem((2 * towers + 2,)),
-            sem((3 + 3 * towers,)),
             sem((1,)),
             sem((1,)),
             sem((2, chips - 1)),
@@ -771,7 +749,7 @@
             sem((3 * towers + 1,)),
         ],
         compiler_params=pltpu.CompilerParams(
-            collective_id=0, has_side_effects=True, vmem_limit_bytes=67043328
+            collective_id=0, has_side_effects=True, vmem_limit_bytes=64 * 10**6
         ),
     )(
         bag_ids[:, 0],
@@ -798,7 +776,8 @@
         ),
         in_specs=[vmem] * 7,
         out_specs=[vmem] * 7,
-    )(*between, accumulator)
+        compiler_params=pltpu.CompilerParams(vmem_limit_bytes=8 * 2**20),
+    )(*(pltpu.with_memory_space_constraint(x, pltpu.VMEM) for x in between), accumulator)
     new_tables, new_acc, grad_first, grad_second, grad_lift, grad_press, logits = out
     return (
         jnp.transpose(new_tables, (0, 2, 1))[:, None],

time: 38.5 us -> 36 us (0.935)
  Pallas kernels: 37.7 us -> 35.1 us
    pallas_call x1, Pallas kernels: 35.3 us -> 34 us  [per_device(): pl.pallas_call(functools.partial(main_kernel, (n, nt)), out_shape=(pltpu....]
    pallas_call x1, Pallas kernels: 2.4 us -> 1.11 us  [per_device(): pl.pallas_call(final_kernel, out_shape=(shape((towers, width, rows), F32)...]
where the time goes in v6:
time: 36 us; the launch traced here: 35.8 us
  Pallas kernels  35.1 us (98%)
  between operations  0.66 us (2%)
    pallas_call x1, Pallas kernels, per_device(): pl.pallas_call(functools.partial(main_kernel, (n, nt)), out_shape=(pltpu....  34 us
    pallas_call x1, Pallas kernels, per_device(): pl.pallas_call(final_kernel, out_shape=(shape((towers, width, rows), F32)...  1.11 us

profile of v6, /device:TPU:1, one launch (start us, length us, event | category | flops | bytes accessed | tf_op | source)
XLA Modules:
  0.0 35.8 jit_solution(13443005806420958447)
XLA Ops:
  0.6 0.0 copy-start
  0.6 34.0 %shard_map.162 = (f32[16,128]{1,0:T(8,128)S(1)}, f32[2,64,512]{2,1,0:T(8,128)S(1)}, f32[2,64,512]{2,1,0:T(8,128)S(1)}, f32[2,64,1024]{2,1,0:T(8,128)S(1)}, f32[2...) custom-call(s32[2,4,512]{2,1,0:T(4,128)} %bitcast.11, s32[2,1,128]{2,1,0:T(1,128)} %touch_ref.1, s32[2,1,128]{2,1,0:T(1,128)} %elapsed_ref.1, ...), custom_call_target="tpu_custom_call" | custom-call | tf_op jit(solution)/shard_map/pallas_call | solution.py:686
  34.6 0.0 copy-done
  34.6 1.1 %shard_map.163 = (f32[2,64,512]{2,1,0:T(8,128)}, f32[2,1,512]{2,1,0:T(1,128)}, f32[64,2,1024]{2,1,0:T(2,128)}, f32[128,2,256]{2,1,0:T(2,128)}, f32[64,128]{1,0:T...) custom-call(f32[16,128]{1,0:T(8,128)S(1)} %get-tuple-element.20.logits_ref, ...), custom_call_target="tpu_custom_call" | custom-call | tf_op jit(solution)/shard_map/pallas_call | solution.py:766
Async XLA Ops:
  0.6 34.0 %copy-start = (f32[2,1,512]{2,1,0:T(1,128)S(1)}, f32[2,1,512]{2,1,0:T(1,128)}, u32[]{:S(2)}) copy-start(f32[2,1,512]{2,1,0:T(1,128)} %acc_ref.1) | copy-start | bytes 12292

commit v7 on v6

--- a/solution.py
+++ b/solution.py
@@ -90,6 +90,8 @@
     act,
     acth,
     actl,
+    ghh,
+    ghl,
     pth,
     ptl,
     gf,
@@ -583,16 +585,15 @@
                 errors[span] * head[:, part]
                 + deep3(split(block), (mixh[:, part], mixl[:, part]))
             )
-            grad_pooled = jnp.zeros((2 * width, chunk), F32)
             for k in range(hid // tile):
                 lanes = slice(k * tile, (k + 1) * tile)
                 grad_act = deep3(go, (w2h[t, lanes, :], w2l[t, lanes, :]), NT)
                 grad_hidden = split(grad_act * stage[t, span, lanes])
-                value = few3((pth[t, :, span], ptl[t, :, span]), grad_hidden)
-                put(gf, (t, slice(None), lanes), value, c == 0)
-                first = (w1h[t, pair_rows, lanes], w1l[t, pair_rows, lanes])
-                grad_pooled = grad_pooled + few3(first, grad_hidden, NT)
-            gpool[t, :, span] = grad_pooled
+                ghh[:, lanes], ghl[:, lanes] = grad_hidden
+            value = few3((pth[t, :, span], ptl[t, :, span]), (ghh[...], ghl[...]))
+            put(gf, (t,), value, c == 0)
+            first = (w1h[t, pair_rows, :], w1l[t, pair_rows, :])
+            gpool[t, :, span] = few3(first, (ghh[...], ghl[...]), NT)
             put(gsec, (t,), deep3((acth[t, :, span], actl[t, :, span]), go), c == 0)
         for copy in back_copies(t):
             copy.start()
@@ -721,6 +722,8 @@
             pltpu.VMEM((half, hid), F32),
             pltpu.VMEM((towers, 2 * block_hid, half), BF16),
             pltpu.VMEM((towers, 2 * block_hid, half), BF16),
+            pltpu.VMEM((min(256, half), hid), BF16),
+            pltpu.VMEM((min(256, half), hid), BF16),
             pltpu.VMEM((towers, 2 * width, half), BF16),
             pltpu.VMEM((towers, 2 * width, half), BF16),
             pltpu.VMEM((towers, 2 * width, hid), F32),

time: 36 us -> 35.5 us (0.986)
  Pallas kernels: 35.1 us -> 34.6 us
    pallas_call x1, Pallas kernels: 34 us -> 33.5 us  [per_device(): pl.pallas_call(functools.partial(main_kernel, (n, nt)), out_shape=(pltpu....]
where the time goes in v7:
time: 35.5 us; the launch traced here: 35.2 us
  Pallas kernels  34.6 us (97%)
  between operations  0.66 us (2%)
    pallas_call x1, Pallas kernels, per_device(): pl.pallas_call(functools.partial(main_kernel, (n, nt)), out_shape=(pltpu....  33.5 us
    pallas_call x1, Pallas kernels, per_device(): pl.pallas_call(final_kernel, out_shape=(shape((towers, width, rows), F32)...  1.11 us

profile of v7, /device:TPU:1, one launch (start us, length us, event | category | flops | bytes accessed | tf_op | source)
XLA Modules:
  0.0 35.2 jit_solution(10605429690637436762)
XLA Ops:
  0.6 0.0 copy-start
  0.6 33.5 %shard_map.162 = (f32[16,128]{1,0:T(8,128)S(1)}, f32[2,64,512]{2,1,0:T(8,128)S(1)}, f32[2,64,512]{2,1,0:T(8,128)S(1)}, f32[2,64,1024]{2,1,0:T(8,128)S(1)}, f32[2...) custom-call(s32[2,4,512]{2,1,0:T(4,128)} %bitcast.11, s32[2,1,128]{2,1,0:T(1,128)} %touch_ref.1, s32[2,1,128]{2,1,0:T(1,128)} %elapsed_ref.1, ...), custom_call_target="tpu_custom_call" | custom-call | tf_op jit(solution)/shard_map/pallas_call | solution.py:687
  34.1 0.0 copy-done
  34.1 1.1 %shard_map.163 = (f32[2,64,512]{2,1,0:T(8,128)}, f32[2,1,512]{2,1,0:T(1,128)}, f32[64,2,1024]{2,1,0:T(2,128)}, f32[128,2,256]{2,1,0:T(2,128)}, f32[64,128]{1,0:T...) custom-call(f32[16,128]{1,0:T(8,128)S(1)} %get-tuple-element.20.logits_ref, ...), custom_call_target="tpu_custom_call" | custom-call | tf_op jit(solution)/shard_map/pallas_call | solution.py:769
Async XLA Ops:
  0.6 33.5 %copy-start = (f32[2,1,512]{2,1,0:T(1,128)S(1)}, f32[2,1,512]{2,1,0:T(1,128)}, u32[]{:S(2)}) copy-start(f32[2,1,512]{2,1,0:T(1,128)} %acc_ref.1) | copy-start | bytes 12292
